TPU v7x, 128 devices: a whole 4x4x4 slice. The times are simulated.
128 devices in a mesh: row: 8 (over y_hi, x), col: 16 (over z, y_lo, core).
Axes of the slice: x: 4, y: 4 (y_hi: 2, y_lo: 2; y = y_hi * 2 + y_lo), z: 4, core: 2. Of those that a mesh axis runs over, the one named last changes fastest.
Arguments:
- features: bfloat16 [64, 1024, 768], P('row', 'col'), may hold values from -6 to 6
- norm_scale: float32 [768], replicated, may hold values from 0.5 to 1.5
- norm_shift: float32 [768], replicated, may hold values from -3 to 3
- expand_weight: bfloat16 [768, 3072], replicated, may hold values from -0.21875 to 0.21875
- expand_bias: float32 [3072], replicated, may hold values from -3 to 3
- depth_kernel: float32 [3, 3, 3072], replicated, may hold values from -2 to 2
- depth_bias: float32 [3072], replicated, may hold values from -3 to 3
- project_weight: bfloat16 [3072, 768], replicated, may hold values from -0.109375 to 0.109375
- project_bias: float32 [768], replicated, may hold values from -2 to 2
- attn_gain: float32 [768], replicated, may hold values from 0.25 to 1.75
- attn_shift: float32 [768], replicated, may hold values from -2 to 2
- qkv_weight: bfloat16 [768, 2304], replicated, may hold values from -0.21875 to 0.21875
- qkv_bias: float32 [2304], replicated, may hold values from -2 to 2
- out_weight: bfloat16 [768, 768], replicated, may hold values from -0.21875 to 0.21875
- out_bias: float32 [768], replicated, may hold values from -2 to 2
Outputs:
- output: bfloat16 [64, 1024, 768], P('row', 'col')
All inputs are finite; a program needn't handle non-finite values.
Results may differ from a plain program's by a relative error of at most 0.006.
Values may be sent and summed in bfloat16 or wider, within the bound.
A program may use at most 192 MiB of HBM per device.

v0:
```python
import math

import jax
import jax.numpy as jnp
from jax import lax
from jax.sharding import PartitionSpec as P

HEADS = 24
HEAD_DIM = 32
GRID = 8


def extended(cells, sides, width):
    for axis, dim in sides:
        count = lax.axis_size(axis)
        ends = count - 1
        head = lax.slice_in_dim(cells, 0, width, axis=dim)
        tail = lax.slice_in_dim(cells, cells.shape[dim] - width, cells.shape[dim], axis=dim)
        cells = jnp.concatenate(
            [
                lax.ppermute(tail, axis, [(i, (i + 1) % count) for i in range(ends)]),
                cells,
                lax.ppermute(head, axis, [((i + 1) % count, i) for i in range(ends)]),
            ],
            axis=dim,
        )
    return cells


def expand_cells(inputs, norm_scale, norm_shift, expand_weight, expand_bias):
    normed = (inputs.astype(jnp.float32) * norm_scale + norm_shift).astype(jnp.bfloat16)
    flat_rows = normed.reshape(-1, normed.shape[-1])
    hidden = jax.nn.gelu(
        jnp.dot(flat_rows, expand_weight, preferred_element_type=jnp.float32) + expand_bias
    )
    return hidden.astype(jnp.bfloat16).reshape(inputs.shape[:-1] + (expand_weight.shape[1],))


def layer_norm(values, scale_vec, shift_vec):
    widened = values.astype(jnp.float32)
    center = widened - jnp.mean(widened, axis=-1, keepdims=True)
    spread = jnp.mean(center * center, axis=-1, keepdims=True)
    return (center * lax.rsqrt(spread + 1e-06) * scale_vec + shift_vec).astype(jnp.bfloat16)


def attend(tokens_in, pattern, qkv_weight, qkv_bias, out_weight, out_bias):
    channels = tokens_in.shape[-1]
    leading = tokens_in.shape[:-1]
    projected = (
        jnp.dot(tokens_in.reshape(-1, channels), qkv_weight, preferred_element_type=jnp.float32)
        + qkv_bias
    )
    projected = projected.astype(jnp.bfloat16).reshape(leading + (3, HEADS, HEAD_DIM))
    query_part = projected[..., 0, :, :]
    key_part = projected[..., 1, :, :]
    value_part = projected[..., 2, :, :]
    renamed = {"i": "m", "j": "n", "k": "o", "l": "p"}
    token_letters = "ijkl"
    key_pattern = "".join((renamed.get(letter, letter) for letter in pattern))
    groups = "".join((letter for letter in pattern if letter not in token_letters))
    query_tokens = "".join((letter for letter in pattern if letter in token_letters))
    key_tokens = "".join((renamed[letter] for letter in query_tokens))
    score_form = groups + "h" + query_tokens + key_tokens
    scores = jnp.einsum(
        pattern + "hd," + key_pattern + "hd->" + score_form,
        query_part,
        key_part,
        preferred_element_type=jnp.float32,
    ) * (1.0 / math.sqrt(HEAD_DIM))
    weights = jnp.exp(scores)
    total = jnp.sum(weights, axis=tuple(range(-len(key_tokens), 0)), keepdims=True)
    probs = (weights / total).astype(jnp.bfloat16)
    mixed = jnp.einsum(
        score_form + "," + key_pattern + "hd->" + pattern + "hd",
        probs,
        value_part,
        preferred_element_type=jnp.float32,
    )
    mixed = mixed.astype(jnp.bfloat16)
    result = (
        jnp.dot(mixed.reshape(-1, channels), out_weight, preferred_element_type=jnp.float32)
        + out_bias
    )
    return result.astype(jnp.bfloat16).reshape(tokens_in.shape)


def per_device(
    features,
    norm_scale,
    norm_shift,
    expand_weight,
    expand_bias,
    depth_kernel,
    depth_bias,
    project_weight,
    project_bias,
    attn_gain,
    attn_shift,
    qkv_weight,
    qkv_bias,
    out_weight,
    out_bias,
):
    tile_rows, tile_cols, channels = features.shape
    row_count = lax.axis_size("row")
    col_count = lax.axis_size("col")
    hidden = expand_cells(features, norm_scale, norm_shift, expand_weight, expand_bias)
    padded = extended(hidden, (("row", 0), ("col", 1)), 1)
    summed = jnp.zeros((tile_rows, tile_cols, padded.shape[-1]), jnp.float32)
    for row_off in range(3):
        for col_off in range(3):
            summed = (
                summed
                + padded[row_off : row_off + tile_rows, col_off : col_off + tile_cols].astype(
                    jnp.float32
                )
                * depth_kernel[row_off, col_off]
            )
    depthwise = jax.nn.gelu(summed + depth_bias).astype(jnp.bfloat16)
    projected = (
        jnp.dot(
            depthwise.reshape(-1, depthwise.shape[-1]),
            project_weight,
            preferred_element_type=jnp.float32,
        )
        + project_bias
    )
    after_conv = (
        features.astype(jnp.float32) + projected.reshape(tile_rows, tile_cols, channels)
    ).astype(jnp.bfloat16)
    attn_in = layer_norm(after_conv, attn_gain, attn_shift)
    fold_row = max(1, GRID // row_count)
    fold_col = max(1, GRID // col_count)
    parity_row = max(1, row_count // GRID)
    parity_col = max(1, col_count // GRID)
    block_row = tile_rows // (fold_row * row_count)
    block_col = tile_cols // (fold_col * col_count)
    tile_view = attn_in.reshape(
        fold_row, row_count, block_row, fold_col, col_count, block_col, channels
    )
    ordered = tile_view.transpose(1, 4, 0, 2, 3, 5, 6).reshape(
        row_count * col_count, fold_row, block_row, fold_col, block_col, channels
    )
    received = lax.all_to_all(ordered, ("row", "col"), split_axis=0, concat_axis=0, tiled=True)
    item_count = received.shape[2]
    grouped = received.reshape(
        row_count // parity_row,
        parity_row,
        col_count // parity_col,
        parity_col,
        fold_row,
        item_count,
        fold_col,
        block_col,
        channels,
    )
    answered = attend(grouped, "jelfiukv", qkv_weight, qkv_bias, out_weight, out_bias).reshape(
        received.shape
    )
    returned = lax.all_to_all(answered, ("row", "col"), split_axis=0, concat_axis=0, tiled=True)
    returned_tiles = returned.reshape(
        row_count, col_count, fold_row, block_row, fold_col, block_col, channels
    ).transpose(2, 0, 3, 4, 1, 5, 6)
    attended = returned_tiles.reshape(tile_rows, tile_cols, channels)
    return (after_conv.astype(jnp.float32) + attended.astype(jnp.float32)).astype(jnp.bfloat16)


def solution(mesh):
    return jax.shard_map(
        per_device,
        mesh=mesh,
        in_specs=(
            P("row", "col", None),
            P(),
            P(),
            P(),
            P(),
            P(),
            P(),
            P(),
            P(),
            P(),
            P(),
            P(),
            P(),
            P(),
            P(),
        ),
        out_specs=P("row", "col", None),
        check_vma=False,
    )
```

profile of v0, /device:TPU:0, one launch (start us, length us, event | category | flops | bytes accessed | tf_op | source)
XLA Modules:
  0.0 198.8 jit_solution(4383727203808470515)
XLA Ops:
  0.0 1.5 fusion.28
  1.5 6.6 %fusion.9 = bf16[512,3072]{1,0:T(8,128)(2,1)S(1)} fusion(bf16[512,768]{1,0:T(8,128)(2,1)S(1)} %bitcast.73, bf16[768,3072]{1,0:T(8,128)(2,1)} %param.18, f32[3072]{0:T(1024)} %param.19), kind=kOutput, calls=%fused_computation.13 | convolution fusion | flops 2431647744 | bytes 8663040 | tf_op jit(solution)/shard_map/dot_general | solution.py:34
  8.2 3.5 %collective-permute-start = (bf16[1,64,3072]{2,1,0:T(8,128)(2,1)S(1)}, bf16[1,64,3072]{2,1,0:T(8,128)(2,1)S(1)}, u32[]{:S(2)}, u32[]{:S(2)}) collective-permute-start(bf16[1,64,3072]{2,1,0:T(8,128)(2,1)S(1)} %get-tuple-element.14), channel_id=1, source_target_pairs={{0,16},{16,32},{32,48},{48,64},{64,80},{80,96},{96,112},{1,17},{17... | collective-permute-start | bytes 1179656 | tf_op jit(solution)/shard_map/ppermute | solution.py:21
  11.7 1.3 collective-permute-start.1
  13.0 7.0 %collective-permute-done = bf16[1,64,3072]{2,1,0:T(8,128)(2,1)S(1)} collective-permute-done((bf16[1,64,3072]{2,1,0:T(8,128)(2,1)S(1)}, bf16[1,64,3072]{2,1,0:T(8,128)(2,1)S(1)}, u32[]{:S(2)}, u32[]{:S(2)}) %collective-permute-start) | collective-permute-done | bytes 393248 | tf_op jit(solution)/shard_map/ppermute | solution.py:21
  20.0 4.1 %collective-permute-done.1 = bf16[1,64,3072]{2,1,0:T(8,128)(2,1)S(1)} collective-permute-done((bf16[1,64,3072]{2,1,0:T(8,128)(2,1)S(1)}, bf16[1,64,3072]{2,1,0:T(8,128)(2,1)S(1)}, u32[]{:S(2)}, u32[]{:S(2)}) %collective-permute-start.1) | collective-permute-done | bytes 393248 | tf_op jit(solution)/shard_map/ppermute | solution.py:23
  24.2 0.2 pad_maximum_fusion.5
  24.4 1.3 collective-permute-start.2
  25.7 1.3 collective-permute-start.3
  27.1 3.6 %collective-permute-done.3 = bf16[10,1,3072]{2,1,0:T(2,128)(2,1)S(1)} collective-permute-done((bf16[10,1,3072]{2,1,0:T(2,128)(2,1)S(1)}, bf16[10,1,3072]{2,1,0:T(2,128)(2,1)S(1)}, u32[]{:S(2)}, u32[]{:S(2)}) %collective-permute-start.3) | collective-permute-done | bytes 61472 | tf_op jit(solution)/shard_map/ppermute | solution.py:23
  30.7 2.3 %maximum_maximum_fusion = (bf16[10,65,3072]{2,1,0:T(8,128)(2,1)S(1)}, bf16[10,65,3072]{2,1,0:T(8,128)(2,1)S(1)}) fusion(bf16[1,64,3072]{2,1,0:T(8,128)(2,1)S(1)} %collective-permute-done.1, bf16[8,64,3072]{2,1,0:T(8,128)(2,1)S(1)} %bitcast.68, bf16[1,64,3072]{2,1,0:T(8,128)(2,1)S(1)} %collective-permute-done, ...), kind=kLoop, calls=%fused_computation.25 | loop fusion | flops 31948800 | bytes 12042240 | tf_op jit(solution)/shard_map/concatenate | solution.py:19
  33.1 9.6 %fusion.17 = bf16[8,64,3072]{2,1,0:T(8,128)(2,1)S(1)} fusion(bf16[8,64,3072]{2,1,0:T(8,128)(2,1)S(1)} %bitcast.69, bf16[10,65,3072]{2,1,0:T(8,128)(2,1)S(1)} %get-tuple-element.11, bf16[1,64,3072]{2,1,0:T(8,128)(2,1)S(1)} %collective-permute-done.1, bf16[10,65,3072]{2,1,0:T(8,128)(2,1)S(1)} %get-tuple-element.10, ...), kind=kLoop, calls=%fused_computation.21 | loop fusion | flops 59768832 | bytes 26075136 | tf_op jit(solution)/shard_map/convert_element_type | solution.py:119
  42.8 2.6 %convolution_add_fusion.1 = f32[512,768]{1,0:T(8,128)S(1)} fusion(bf16[512,3072]{1,0:T(8,128)(2,1)S(1)} %bitcast.71, bf16[3072,768]{1,0:T(8,128)(2,1)S(1)} %bitcast.84, f32[768]{0:T(1024)S(1)} %copy-done.9), kind=kOutput, calls=%fused_computation.50 | convolution fusion | flops 2416312320 | bytes 9440256 | tf_op jit(solution)/shard_map/dot_general | solution.py:121
  45.4 0.3 convert_reduce_fusion
  45.7 0.3 fusion.23
  46.1 0.5 copy-done.2
  46.6 1.2 fusion.26
  47.8 2.4 %reshape_transpose_reshape.4 = bf16[128,1,1,1,4,768]{5,4,3,2,1,0:T(4,128)(2,1)} reshape(bf16[8,64,768]{2,1,0:T(8,128)(2,1)} %fusion.26) | data formatting | bytes 1572864 | tf_op jit(solution)/shard_map/reshape;transpose;reshape | solution.py:141
  50.2 34.3 %all_to_all.10 = bf16[128,1,1,1,4,768]{5,4,3,2,1,0:T(4,128)(2,1)} all-to-all(bf16[128,1,1,1,4,768]{5,4,3,2,1,0:T(4,128)(2,1)} %reshape_transpose_reshape.4), channel_id=1, replica_groups=mesh['row'=8,'col'=16] {'row','col'}, dimensions={0} | all-to-all | bytes 1572864 | tf_op jit(solution)/shard_map/all_to_all | solution.py:144
  84.5 2.3 %reshape_reshape.6 = bf16[512,768]{1,0:T(8,128)(2,1)} reshape(bf16[128,1,1,1,4,768]{5,4,3,2,1,0:T(4,128)(2,1)} %all_to_all.10) | data formatting | bytes 1572864 | tf_op jit(solution)/shard_map/reshape;reshape | solution.py:50
  86.8 4.5 %fusion.18 = bf16[512,2304]{1,0:T(8,128)(2,1)} fusion(bf16[512,768]{1,0:T(8,128)(2,1)} %reshape_reshape.6, bf16[768,2304]{1,0:T(8,128)(2,1)S(1)} %copy-done, f32[2304]{0:T(1024)S(1)} %copy-done.8), kind=kOutput, calls=%fused_computation.24 | convolution fusion | flops 1814298624 | bytes 6693888 | tf_op jit(solution)/shard_map/dot_general | solution.py:50
  91.3 11.6 %reshape.73 = bf16[8,1,8,2,1,1,1,4,3,24,32]{10,9,8,7,3,2,0,6,5,4,1:T(8,128)(2,1)} reshape(bf16[512,2304]{1,0:T(8,128)(2,1)} %fusion.18) | data formatting | bytes 4718592 | tf_op jit(solution)/shard_map/reshape | solution.py:53
  102.9 5.8 %fusion.33 = (bf16[8,1,8,2,1,1,1,4,1,24,32]{10,9,8,7,3,2,0,6,5,4,1:T(8,128)(2,1)}, bf16[8,1,8,2,1,1,1,4,1,24,32]{10,9,8,7,3,2,0,6,5,4,1:T(8,128)(2,1)S(1)}, bf16[8,1,8,2,1,1,1,4,1,24,32]{10,9,8,7,3,2,0,6,5,4,1:T(8,128)(2,1)S(1)}) fusion(bf16[8,1,8,2,1,1,1,4,3,24,32]{10,9,8,7,3,2,0,6,5,4,1:T(8,128)(2,1)} %reshape.73), kind=kLoop, calls=%fused_computation.59 | loop fusion | bytes 4718592 | tf_op jit(solution)/shard_map/slice | solution.py:56
  108.7 26.6 %fusion = (f32[2,4,24,8,8]{4,3,2,1,0:T(8,128)}, f32[2,4,24,8,8,8,8]{4,6,5,3,2,1,0:T(8,128)}) fusion(bf16[8,1,8,2,1,1,1,4,1,24,32]{10,9,8,7,3,2,0,6,5,4,1:T(8,128)(2,1)S(1)} %get-tuple-element.9, bf16[8,1,8,2,1,1,1,4,1,24,32]{10,9,8,7,3,2,0,6,5,4,1:T(8,128)(2,1)S(1)} %get-tuple-element.8), kind=kOutput, calls=%fused_computation.2 | convolution fusion | flops 51892224 | bytes 4767744 | tf_op jit(solution)/shard_map/jelfiukvhd,nepfmuovhd->efuvhjliknpmo/dot_general | solution.py:64
  135.3 24.3 %fusion.19 = bf16[8,1,8,2,1,1,1,4,24,32]{9,2,0,8,7,3,6,4,5,1:T(8,128)(2,1)} fusion(f32[2,4,24,8,8,8,8]{4,6,5,3,2,1,0:T(8,128)} %get-tuple-element.26, f32[2,4,24,8,8]{4,3,2,1,0:T(8,128)} %get-tuple-element.25, bf16[8,1,8,2,1,1,1,4,1,24,32]{10,9,8,7,3,2,0,6,5,4,1:T(8,128)(2,1)} %get-tuple-element.7), kind=kOutput, calls=%fused_computation.27 | convolution fusion | flops 53084160 | bytes 4767744 | tf_op jit(solution)/shard_map/efuvhjliknpmo,nepfmuovhd->jelfiukvhd/dot_general | solution.py:73
  159.6 3.9 %copy.29 = bf16[8,1,8,2,1,1,1,4,24,32]{9,8,7,3,2,0,6,5,4,1:T(8,128)(2,1)S(1)} copy(bf16[8,1,8,2,1,1,1,4,24,32]{9,2,0,8,7,3,6,4,5,1:T(8,128)(2,1)} %fusion.19) | data formatting | bytes 1572864 | tf_op jit(solution)/shard_map/convert_element_type | solution.py:79
  163.5 2.8 %reshape.77 = bf16[512,768]{1,0:T(8,128)(2,1)} reshape(bf16[8,1,8,2,1,1,1,4,24,32]{9,8,7,3,2,0,6,5,4,1:T(8,128)(2,1)S(1)} %copy.29) | data formatting | bytes 1572864 | tf_op jit(solution)/shard_map/reshape | solution.py:81
  166.3 3.3 %add_convert_fusion = bf16[512,768]{1,0:T(8,128)(2,1)} fusion(bf16[512,768]{1,0:T(8,128)(2,1)} %reshape.77, bf16[768,768]{1,0:T(8,128)(2,1)} %param.28, f32[768]{0:T(1024)S(1)} %copy-done.10), kind=kOutput, calls=%fused_computation.49 | convolution fusion | flops 604766208 | bytes 2755584 | tf_op jit(solution)/shard_map/dot_general | solution.py:81
  169.7 2.4 %reshape_reshape.7 = bf16[128,1,1,1,4,768]{5,4,0,3,2,1:T(4,128)(2,1)} reshape(bf16[512,768]{1,0:T(8,128)(2,1)} %add_convert_fusion) | data formatting | bytes 1572864 | tf_op jit(solution)/shard_map/reshape;reshape | solution.py:157
  172.0 21.6 %all_to_all.11 = bf16[128,1,1,1,4,768]{5,4,3,2,1,0:T(4,128)(2,1)} all-to-all(bf16[128,1,1,1,4,768]{5,4,3,2,1,0:T(4,128)(2,1)} %bitcast.70), channel_id=1, replica_groups=mesh['row'=8,'col'=16] {'row','col'}, dimensions={0} | all-to-all | bytes 1572864 | tf_op jit(solution)/shard_map/all_to_all | solution.py:160
  193.7 2.5 %reshape.78 = f32[8,64,768]{2,1,0:T(8,128)} reshape(bf16[128,1,1,1,4,768]{5,4,3,2,1,0:T(4,128)(2,1)} %all_to_all.11) | data formatting | bytes 2359296 | tf_op jit(solution)/shard_map/convert_element_type | solution.py:165
  196.2 2.7 %fusion.30 = bf16[8,64,768]{2,1,0:T(8,128)(2,1)} fusion(f32[8,64,768]{2,1,0:T(8,128)} %reshape.78, bf16[8,64,768]{2,1,0:T(8,128)(2,1)} %copy-done.2), kind=kLoop, calls=%fused_computation.48 | loop fusion | flops 1179648 | bytes 3145728 | tf_op jit(solution)/shard_map/convert_element_type | solution.py:165
  (31 shorter events, 0.2 us)
Async XLA Ops:
  0.0 86.8 %copy-start = (bf16[768,2304]{1,0:T(8,128)(2,1)S(1)}, bf16[768,2304]{1,0:T(8,128)(2,1)}, u32[]{:S(2)}) copy-start(bf16[768,2304]{1,0:T(8,128)(2,1)} %param.26) | copy-start | bytes 10616836
  8.1 18.9 %copy-start.4 = (f32[3,3,3072]{2,1,0:T(4,128)S(1)}, f32[3,3,3072]{2,1,0:T(4,128)}, u32[]{:S(2)}) copy-start(f32[3,3,3072]{2,1,0:T(4,128)} %param.20) | copy-start | bytes 331780
  8.2 11.8 %collective-permute-start = (bf16[1,64,3072]{2,1,0:T(8,128)(2,1)S(1)}, bf16[1,64,3072]{2,1,0:T(8,128)(2,1)S(1)}, u32[]{:S(2)}, u32[]{:S(2)}) collective-permute-start(bf16[1,64,3072]{2,1,0:T(8,128)(2,1)S(1)} %get-tuple-element.14), channel_id=1, source_target_pairs={{0,16},{16,32},{32,48},{48,64},{64,80},{80,96},{96,112},{1,17},{17... | collective-permute-start | bytes 1179656 | tf_op jit(solution)/shard_map/ppermute | solution.py:21
  11.7 12.5 %collective-permute-start.1 = (bf16[1,64,3072]{2,1,0:T(8,128)(2,1)S(1)}, bf16[1,64,3072]{2,1,0:T(8,128)(2,1)S(1)}, u32[]{:S(2)}, u32[]{:S(2)}) collective-permute-start(bf16[1,64,3072]{2,1,0:T(8,128)(2,1)S(1)} %get-tuple-element.15), channel_id=1, source_target_pairs={{16,0},{32,16},{48,32},{64,48},{80,64},{96,80},{112,96},{17,1},{33... | collective-permute-start | bytes 1179656 | tf_op jit(solution)/shard_map/ppermute | solution.py:23
  24.4 2.7 %collective-permute-start.2 = (bf16[10,1,3072]{2,1,0:T(2,128)(2,1)S(1)}, bf16[10,1,3072]{2,1,0:T(2,128)(2,1)S(1)}, u32[]{:S(2)}, u32[]{:S(2)}) collective-permute-start(bf16[10,1,3072]{2,1,0:T(2,128)(2,1)S(1)} %get-tuple-element.12), channel_id=1, source_target_pairs={{0,1},{1,2},{2,3},{3,4},{4,5},{5,6},{6,7},{7,8},{8,9},{9,10},{10,1... | collective-permute-start | bytes 184328 | tf_op jit(solution)/shard_map/ppermute | solution.py:21
  25.7 5.0 %collective-permute-start.3 = (bf16[10,1,3072]{2,1,0:T(2,128)(2,1)S(1)}, bf16[10,1,3072]{2,1,0:T(2,128)(2,1)S(1)}, u32[]{:S(2)}, u32[]{:S(2)}) collective-permute-start(bf16[10,1,3072]{2,1,0:T(2,128)(2,1)S(1)} %get-tuple-element.13), channel_id=1, source_target_pairs={{1,0},{2,1},{3,2},{4,3},{5,4},{6,5},{7,6},{8,7},{9,8},{10,9},{11,1... | collective-permute-start | bytes 184328 | tf_op jit(solution)/shard_map/ppermute | solution.py:23
  27.1 5.9 %copy-start.5 = (f32[3072]{0:T(1024)S(1)}, f32[3072]{0:T(1024)}, u32[]{:S(2)}) copy-start(f32[3072]{0:T(1024)} %param.21) | copy-start | bytes 36868
  30.7 12.0 %slice-start = ((s8[4718592]{0:T(1024)(128)(4,1)}), s8[4194304]{0:T(1024)(128)(4,1)S(1)}, s32[]{:S(2)}) async-start(s8[4718592]{0:T(1024)(128)(4,1)} %bitcast.83), calls=%async_computation.2 | async-start | bytes 8388608
  33.0 9.7 %slice-start.1 = ((s8[4718592]{0:T(1024)(128)(4,1)}), s8[524288]{0:T(1024)(128)(4,1)S(1)}, s32[]{:S(2)}) async-start(s8[4718592]{0:T(1024)(128)(4,1)} %bitcast.83), calls=%async_computation.3 | async-start | bytes 1048576
  33.0 9.7 %copy-start.9 = (f32[768]{0:T(1024)S(1)}, f32[768]{0:T(1024)}, u32[]{:S(2)}) copy-start(f32[768]{0:T(1024)} %param.23) | copy-start | bytes 9220
  42.7 2.7 %copy-start.3 = (bf16[8,64,768]{2,1,0:T(8,128)(2,1)S(1)}, bf16[8,64,768]{2,1,0:T(8,128)(2,1)}, u32[]{:S(2)}) copy-start(bf16[8,64,768]{2,1,0:T(8,128)(2,1)} %param.15) | copy-start | bytes 2359300
  42.7 3.8 %copy-start.6 = (f32[768]{0:T(1024)S(1)}, f32[768]{0:T(1024)}, u32[]{:S(2)}) copy-start(f32[768]{0:T(1024)} %param.25) | copy-start | bytes 9220
  42.8 3.8 %copy-start.7 = (f32[768]{0:T(1024)S(1)}, f32[768]{0:T(1024)}, u32[]{:S(2)}) copy-start(f32[768]{0:T(1024)} %param.24) | copy-start | bytes 9220
  45.4 41.4 %copy-start.8 = (f32[2304]{0:T(1024)S(1)}, f32[2304]{0:T(1024)}, u32[]{:S(2)}) copy-start(f32[2304]{0:T(1024)} %param.27) | copy-start | bytes 27652
  45.7 0.9 copy-start.2
  159.6 6.7 %copy-start.10 = (f32[768]{0:T(1024)S(1)}, f32[768]{0:T(1024)}, u32[]{:S(2)}) copy-start(f32[768]{0:T(1024)} %param.29) | copy-start | bytes 9220
  166.3 32.5 %copy-start.1 = (bf16[768,2304]{1,0:T(8,128)(2,1)S(1)}, bf16[768,2304]{1,0:T(8,128)(2,1)}, u32[]{:S(2)}) copy-start(bf16[768,2304]{1,0:T(8,128)(2,1)} %param.26) | copy-start | bytes 10616836
where the time goes:
time: 200 us; the launch traced here: 199 us
  matrix products  68 us (34%)
  blocking collectives  56 us (28%)
  local copies, waits for them, and re-layouts  34.3 us (17%)
  other arithmetic  18.1 us (9%)
  waiting for transfers between devices  14.8 us (7%)
  starting transfers between devices  7.38 us (4%)
    all_to_all x1, blocking collectives, per_device(): lax.all_to_all(ordered, ('row', 'col'), split_axis=0, concat_axis=0, tile...  34.3 us
    dot_general x1, matrix products, attend(): jnp.einsum(pattern + 'hd,' + key_pattern + 'hd->' + score_form, query_par...  26.6 us
    dot_general x1, matrix products, attend(): jnp.einsum(score_form + ',' + key_pattern + 'hd->' + pattern + 'hd', prob...  24.3 us
    all_to_all x1, blocking collectives, per_device(): lax.all_to_all(answered, ('row', 'col'), split_axis=0, concat_axis=0, til...  21.6 us
    reshape x1, local copies, waits for them, and re-layouts, attend(): projected.astype(jnp.bfloat16).reshape(leading + (3, HEADS, HEAD_DIM))  11.6 us
    convert_element_type x1, other arithmetic, per_device(): depthwise = jax.nn.gelu(summed + depth_bias).astype(jnp.bfloat16)  9.63 us
    ppermute x2, waiting for transfers between devices, extended(): lax.ppermute(head, axis, [((i + 1) % count, i) for i in range(ends)])  7.76 us
    ppermute x2, waiting for transfers between devices, extended(): lax.ppermute(tail, axis, [(i, (i + 1) % count) for i in range(ends)])  7.04 us
  transfers between devices with their start and end apart: 4, of which 3 were waited for; matrix products, arithmetic and copies ran while one was open for 0% of the time, Pallas kernels for 0%

commit v1 on v0

v1 whole, which is shorter than its diff:
```python
import math

import jax
import jax.numpy as jnp
from jax import lax
from jax.experimental import pallas as pl
from jax.experimental.pallas import tpu as pltpu
from jax.sharding import PartitionSpec as P

MESH = pl.DeviceIdType.MESH
F32 = jnp.float32
BF16 = jnp.bfloat16

ROWS, COLS = 8, 16
PEERS = 64
TR, TC = 8, 64
TOKENS = TR * TC
C = 768
E = 3072
HEAD_DIM = 32
QUADS = 6
NQ = 2
WCHUNKS = 6
GC1 = math.sqrt(2.0 / math.pi)
GC2 = GC1 * 0.044715
EXP_SCALE = math.log2(math.e) / math.sqrt(HEAD_DIM)


def gelu(v):
    half = 0.5 * v
    return half + half * jnp.tanh(v * (GC1 + GC2 * (v * v)))


def kernel(
    f_hbm, nsc_h, nsh_h, we_h, be_h, dk_h, db_h, wp_h, bp_h, ag_h, as_h, wq_h, bq_h, wo_h, bo_h,
    ac_out, ret_out,
    feat, nsc, nsh, we, be, dk, db, wp, bp, ag, ash, wq, bq, wo, bo,
    xn, top, bot, left, right, corner, xblk, xcol, hid, hl, hr, dwb, send, recv, xp, qkv, mixed, retbuf, ones,
    small_sem, feat_sem, we_sem, w_sem, halo_ssem, halo_rsem, a_ssem, a_rsem, b_ssem, b_rsem, out_sem, self_sem,
):
    r = lax.axis_index("row")
    c = lax.axis_index("col")
    core = lax.rem(c, 2)
    me = r * 8 + c // 2

    def place(p):
        return (p // 8, 2 * lax.rem(p, 8) + core)

    bar = pltpu.get_barrier_semaphore()

    fcopy = pltpu.make_async_copy(f_hbm, feat, feat_sem)
    fcopy.start()
    smalls = [
        pltpu.make_async_copy(s, d, small_sem.at[i])
        for i, (s, d) in enumerate(
            ((nsc_h, nsc), (nsh_h, nsh), (be_h, be), (dk_h, dk), (db_h, db), (bp_h, bp),
             (ag_h, ag), (as_h, ash), (bq_h, bq), (bo_h, bo))
        )
    ]
    for s in smalls:
        s.start()
    wide = E // WCHUNKS
    wcopies = [
        pltpu.make_async_copy(
            we_h.at[:, pl.ds(i * wide, wide)], we.at[:, pl.ds(i * wide, wide)], we_sem.at[i]
        )
        for i in range(WCHUNKS)
    ]
    for w in wcopies:
        w.start()

    def signal(i, _):
        pl.semaphore_signal(
            bar, inc=1, device_id=place(lax.rem(me + i, PEERS)), device_id_type=MESH
        )
        return 0

    lax.fori_loop(1, PEERS, signal, 0)
    for dr in (-1, 0, 1):
        for dc in (-1, 1):
            pl.semaphore_signal(
                bar, inc=1,
                device_id=(lax.rem(r + dr + ROWS, ROWS), lax.rem(c + dc + COLS, COLS)),
                device_id_type=MESH,
            )

    bigs = [
        pltpu.make_async_copy(s, d, w_sem.at[i])
        for i, (s, d) in enumerate(((wp_h, wp), (wq_h, wq), (wo_h, wo)))
    ]
    for w in bigs:
        w.start()

    fcopy.wait()
    for s in smalls:
        s.wait()

    def normalise(v):
        return (v.astype(F32) * nsc[...] + nsh[...]).astype(BF16)

    def norm_row(h, _):
        xn[pl.ds(pl.multiple_of(h * TC, TC), TC), :] = normalise(feat[h])
        return 0

    lax.fori_loop(0, TR, norm_row, 0)

    def expand_chunk(ci, _):
        cols = pl.ds(pl.multiple_of(ci * 256, 256), 256)
        for mb in range(2):
            acc = jnp.dot(
                xn[mb * 256 : (mb + 1) * 256, :], we[:, cols], preferred_element_type=F32
            )
            g = gelu(acc + be[:, cols]).astype(BF16)
            hid[1 + 4 * mb : 5 + 4 * mb, :, cols] = g.reshape(4, TC, 256)
        return 0

    early = 4
    for i in range(early):
        wcopies[i].wait()
        lax.fori_loop(2 * i, 2 * i + 2, expand_chunk, 0)

    pl.semaphore_wait(bar, PEERS - 1 + 6)

    def halo(src, dst, k, dr, dc):
        return pltpu.make_async_remote_copy(
            src_ref=src, dst_ref=dst, send_sem=halo_ssem.at[k], recv_sem=halo_rsem.at[k],
            device_id=(lax.rem(r + dr + ROWS, ROWS), lax.rem(c + dc + COLS, COLS)),
            device_id_type=MESH,
        )

    halos = [
        halo(feat.at[TR - 1], top, 0, 1, 0),
        halo(feat.at[0], bot, 1, -1, 0),
        halo(feat.at[:, pl.ds(TC - 8, 8)], left, 2, 0, 1),
        halo(feat.at[:, pl.ds(0, 8)], right, 3, 0, -1),
        halo(feat.at[TR - 1, pl.ds(TC - 8, 8)], corner.at[0], 4, 1, 1),
        halo(feat.at[0, pl.ds(TC - 8, 8)], corner.at[1], 5, -1, 1),
        halo(feat.at[TR - 1, pl.ds(0, 8)], corner.at[2], 6, 1, -1),
        halo(feat.at[0, pl.ds(0, 8)], corner.at[3], 7, -1, -1),
    ]
    for h in halos:
        h.start()

    for i in range(early, WCHUNKS):
        wcopies[i].wait()
        lax.fori_loop(2 * i, 2 * i + 2, expand_chunk, 0)

    for h in halos:
        h.wait()

    top_ok = jnp.where(r > 0, 1.0, 0.0).astype(F32)
    bot_ok = jnp.where(r < ROWS - 1, 1.0, 0.0).astype(F32)
    left_ok = jnp.where(c > 0, 1.0, 0.0).astype(F32)
    right_ok = jnp.where(c < COLS - 1, 1.0, 0.0).astype(F32)

    xn[0:TC, :] = normalise(top[...])
    xn[TC : 2 * TC, :] = normalise(bot[...])
    for i in range(TR):
        xblk[i * 8 : i * 8 + 8, :] = normalise(left[i])
        xblk[64 + i * 8 : 64 + i * 8 + 8, :] = normalise(right[i])
    for i in range(4):
        xblk[128 + i * 8 : 136 + i * 8, :] = normalise(corner[i])
    xblk[160:256, :] = jnp.zeros((96, C), BF16)
    t = lax.broadcasted_iota(jnp.int32, (32, 256), 0)
    n = lax.broadcasted_iota(jnp.int32, (32, 256), 1)
    tr = lax.rem(t, 16)
    want_l = jnp.where(tr == 0, 135, jnp.where(tr == 9, 143, (tr - 1) * 8 + 7))
    want_r = jnp.where(tr == 0, 144, jnp.where(tr == 9, 152, 64 + (tr - 1) * 8))
    want = jnp.where(t < 16, want_l, want_r)
    want = jnp.where(tr <= 9, want, -1)
    pick = jnp.where(n == want, 1.0, 0.0).astype(BF16)
    xcol[...] = jnp.dot(pick, xblk[...], preferred_element_type=F32).astype(BF16)

    def halo_chunk(ci, _):
        cols = pl.ds(pl.multiple_of(ci * 256, 256), 256)
        acc = jnp.dot(xn[0 : 2 * TC, :], we[:, cols], preferred_element_type=F32)
        g = gelu(acc + be[:, cols])
        hid[0, :, cols] = (g[0:TC] * top_ok).astype(BF16)
        hid[TR + 1, :, cols] = (g[TC : 2 * TC] * bot_ok).astype(BF16)
        side = jnp.dot(xcol[...], we[:, cols], preferred_element_type=F32)
        gs = gelu(side + be[:, cols]).astype(BF16).astype(F32)
        ti = lax.broadcasted_iota(jnp.int32, (16, 256), 0)
        edge = jnp.where(ti == 0, top_ok, jnp.where(ti == 9, bot_ok, 1.0))
        gl = gs[0:16] * (edge * left_ok)
        gr = gs[16:32] * (edge * right_ok)
        kl = [dk[a, 0:1, cols] for a in range(3)]
        kr = [dk[a, 2:3, cols] for a in range(3)]
        ledge = gl[0:8] * kl[0] + gl[1:9] * kl[1] + gl[2:10] * kl[2]
        redge = gr[0:8] * kr[0] + gr[1:9] * kr[1] + gr[2:10] * kr[2]
        for i in range(TR):
            hl[i, :, cols] = jnp.broadcast_to(ledge[i : i + 1], (8, 256))
            hr[i, :, cols] = jnp.broadcast_to(redge[i : i + 1], (8, 256))
        return 0

    lax.fori_loop(0, E // 256, halo_chunk, 0)

    bigs[0].wait()
    sub_id = lax.broadcasted_iota(jnp.int32, (8, 128), 0)

    def send_chunk(p):
        return pltpu.make_async_remote_copy(
            src_ref=send.at[p], dst_ref=recv.at[me], send_sem=a_ssem, recv_sem=a_rsem,
            device_id=place(p), device_id_type=MESH,
        )

    def block(k, _):
        b = lax.rem(k + me, 4)

        def lane(ci, _):
            cols = pl.ds(pl.multiple_of(ci * 128, 128), 128)
            rows = [hid[2 * b + i, :, cols].astype(F32) for i in range(4)]
            bias = db[:, cols]
            taps = [[dk[a, q : q + 1, cols] for q in range(3)] for a in range(3)]
            for o in range(2):
                s = [
                    rows[o] * taps[0][q] + rows[o + 1] * taps[1][q] + rows[o + 2] * taps[2][q]
                    for q in range(3)
                ]
                down = pltpu.roll(s[0], 1, 0)
                up = pltpu.roll(s[2], TC - 1, 0)
                first = jnp.where(sub_id == 0, hl[2 * b + o, :, cols], down[0:8])
                last = jnp.where(sub_id == 7, hr[2 * b + o, :, cols], up[TC - 8 : TC])
                total = (
                    s[1] + bias
                    + jnp.concatenate([first, down[8:TC]], axis=0)
                    + jnp.concatenate([up[0 : TC - 8], last], axis=0)
                )
                dwb[o * TC : (o + 1) * TC, cols] = gelu(total).astype(BF16)
            return 0

        lax.fori_loop(0, E // 128, lane, 0)
        proj = jnp.dot(dwb[...], wp[...], preferred_element_type=F32) + bp[...]
        f0 = feat[2 * b].astype(F32)
        f1 = feat[2 * b + 1].astype(F32)
        for o, f in ((0, f0), (1, f1)):
            acb = (f + proj[o * TC : (o + 1) * TC]).astype(BF16)
            feat[2 * b + o] = acb
            wide_ac = acb.astype(F32)
            center = wide_ac - jnp.mean(wide_ac, axis=-1, keepdims=True)
            spread = jnp.mean(center * center, axis=-1, keepdims=True)
            y = (center * lax.rsqrt(spread + 1e-06) * ag[...] + ash[...]).astype(BF16)
            send[pl.ds((2 * b + o) * 8, 8)] = y.reshape(8, 8, C)

        def go(j, _):
            p = 16 * b + lax.rem(j + me, 16)

            @pl.when(p != me)
            def _():
                send_chunk(p).start()

            return 0

        lax.fori_loop(0, 16, go, 0)
        return 0

    lax.fori_loop(0, 4, block, 0)
    accopy = pltpu.make_async_copy(feat, ac_out, out_sem)
    accopy.start()
    recv[pl.ds(me, 1)] = send[pl.ds(me, 1)]
    ri = lax.broadcasted_iota(jnp.int32, (256, 256), 0) // 64
    rj = lax.broadcasted_iota(jnp.int32, (256, 256), 1) // 64
    ones[...] = jnp.where(ri == rj, 1.0, 0.0).astype(BF16)
    bigs[1].wait()
    bigs[2].wait()
    pltpu.make_async_copy(send.at[pl.ds(0, PEERS - 1)], send.at[pl.ds(0, PEERS - 1)], a_ssem).wait()
    pltpu.make_async_copy(recv.at[pl.ds(0, PEERS - 1)], recv.at[pl.ds(0, PEERS - 1)], a_rsem).wait()

    x = recv[...].reshape(TOKENS, C)
    for mb in range(2):
        m = lax.broadcasted_iota(jnp.int32, (256, TOKENS), 0) + mb * 256
        nn = lax.broadcasted_iota(jnp.int32, (256, TOKENS), 1)
        perm = jnp.where(nn == lax.rem(m, 64) * 8 + m // 64, 1.0, 0.0).astype(BF16)
        xp[mb * 256 : (mb + 1) * 256, :] = jnp.dot(perm, x, preferred_element_type=F32).astype(BF16)

    def qkv_chunk(ci, _):
        cols = pl.ds(pl.multiple_of(ci * 256, 256), 256)
        for mb in range(2):
            acc = jnp.dot(
                xp[mb * 256 : (mb + 1) * 256, :], wq[:, cols], preferred_element_type=F32
            )
            qkv[mb * 256 : (mb + 1) * 256, cols] = (acc + bq[:, cols]).astype(BF16)
        return 0

    lax.fori_loop(0, 9, qkv_chunk, 0)

    per = PEERS // NQ
    lane_head = lax.broadcasted_iota(jnp.int32, (64, 128), 1) // HEAD_DIM
    masks = [jnp.where(lane_head == i, 1.0, 0.0).astype(BF16) for i in range(4)]

    def return_chunk(p):
        return pltpu.make_async_remote_copy(
            src_ref=retbuf.at[p], dst_ref=ret_out.at[me], send_sem=b_ssem, recv_sem=b_rsem,
            device_id=place(p), device_id_type=MESH,
        )

    def query_block(qq, _):
        qb = lax.rem(qq + me, NQ)

        def group(g, _):
            krows = pl.ds(pl.multiple_of(g * 64, 64), 64)
            qrows = pl.ds(pl.multiple_of(g * 64 + qb * per, per), per)
            orows = pl.ds(pl.multiple_of(g * per, per), per)
            for quad in range(QUADS):
                lo = quad * 128
                q = qkv[qrows, lo : lo + 128]
                kk = qkv[krows, C + lo : C + lo + 128]
                vv = qkv[krows, 2 * C + lo : 2 * C + lo + 128]
                kbd = jnp.concatenate([kk * m for m in masks], axis=0)
                vbd = jnp.concatenate([vv * m for m in masks], axis=0)
                s = lax.dot_general(
                    q, kbd, (((1,), (1,)), ((), ())), preferred_element_type=F32
                )
                e = jnp.exp2(s * EXP_SCALE)
                tot = jnp.dot(e.astype(BF16), ones[...], preferred_element_type=F32)
                probs = (e / tot).astype(BF16)
                o = jnp.dot(probs, vbd, preferred_element_type=F32)
                mixed[orows, lo : lo + 128] = o.astype(BF16)
            return 0

        lax.fori_loop(0, 8, group, 0)
        rows = per * 8
        m = lax.broadcasted_iota(jnp.int32, (rows, rows), 0)
        nn = lax.broadcasted_iota(jnp.int32, (rows, rows), 1)
        back = jnp.where(nn == lax.rem(m, 8) * per + m // 8, 1.0, 0.0).astype(BF16)
        mm = jnp.dot(back, mixed[...], preferred_element_type=F32).astype(BF16)
        y = (jnp.dot(mm, wo[...], preferred_element_type=F32) + bo[...]).astype(BF16)
        retbuf[pl.ds(qb * per, per)] = y.reshape(per, 8, C)

        def go(j, _):
            p = per * qb + lax.rem(j + me, per)

            @pl.when(p != me)
            def _():
                return_chunk(p).start()

            return 0

        lax.fori_loop(0, per, go, 0)
        return 0

    lax.fori_loop(0, NQ, query_block, 0)
    own = pltpu.make_async_copy(retbuf.at[me], ret_out.at[me], self_sem)
    own.start()
    own.wait()
    accopy.wait()
    pltpu.make_async_copy(retbuf.at[pl.ds(0, PEERS - 1)], retbuf.at[pl.ds(0, PEERS - 1)], b_ssem).wait()
    pltpu.make_async_copy(
        ret_out.at[pl.ds(0, PEERS - 1)], ret_out.at[pl.ds(0, PEERS - 1)], b_rsem
    ).wait()


def per_device(
    features, norm_scale, norm_shift, expand_weight, expand_bias, depth_kernel, depth_bias,
    project_weight, project_bias, attn_gain, attn_shift, qkv_weight, qkv_bias, out_weight, out_bias,
):
    row = lambda v: v.reshape(1, -1)
    args = (
        features, row(norm_scale), row(norm_shift), expand_weight, row(expand_bias), depth_kernel,
        row(depth_bias), project_weight, row(project_bias), row(attn_gain), row(attn_shift),
        qkv_weight, row(qkv_bias), out_weight, row(out_bias),
    )
    vm = pltpu.VMEM
    dma = pltpu.SemaphoreType.DMA
    scratch = [vm(a.shape, a.dtype) for a in args]
    scratch += [
        vm((TOKENS, C), BF16),
        vm((TC, C), BF16),
        vm((TC, C), BF16),
        vm((TR, 8, C), BF16),
        vm((TR, 8, C), BF16),
        vm((4, 8, C), BF16),
        vm((256, C), BF16),
        vm((32, C), BF16),
        vm((TR + 2, TC, E), BF16),
        vm((TR, 8, E), F32),
        vm((TR, 8, E), F32),
        vm((2 * TC, E), BF16),
        vm((PEERS, 8, C), BF16),
        vm((PEERS, 8, C), BF16),
        vm((TOKENS, C), BF16),
        vm((TOKENS, 3 * C), BF16),
        vm((TOKENS // NQ, C), BF16),
        vm((PEERS, 8, C), BF16),
        vm((256, 256), BF16),
        dma((10,)), dma, dma((WCHUNKS,)), dma((3,)), dma((8,)), dma((8,)),
        dma, dma, dma, dma, dma, dma,
    ]
    hbm = pl.BlockSpec(memory_space=pl.ANY)
    after_conv, attended = pl.pallas_call(
        kernel,
        out_shape=(
            jax.ShapeDtypeStruct((TR, TC, C), BF16),
            jax.ShapeDtypeStruct((PEERS, 8, C), BF16),
        ),
        in_specs=[hbm] * len(args),
        out_specs=(hbm, hbm),
        scratch_shapes=scratch,
        name="block",
        compiler_params=pltpu.CompilerParams(
            collective_id=0, has_side_effects=True, vmem_limit_bytes=60 << 20
        ),
    )(*args)
    return (after_conv.astype(F32) + attended.reshape(after_conv.shape).astype(F32)).astype(BF16)


def solution(mesh):
    return jax.shard_map(
        per_device,
        mesh=mesh,
        in_specs=(P("row", "col", None),) + (P(),) * 14,
        out_specs=P("row", "col", None),
        check_vma=False,
    )
```

time: 200 us -> 87.1 us (0.44)
  Pallas kernels: 0 us -> 75.4 us
  matrix products: 68 us -> 0 us
  blocking collectives: 56 us -> 0 us
  local copies, waits for them, and re-layouts: 34.3 us -> 8.95 us
  other arithmetic: 18.1 us -> 2.43 us
  waiting for transfers between devices: 14.8 us -> 0 us
  starting transfers between devices: 7.38 us -> 0 us
    pallas_call x0 -> x1, Pallas kernels: none -> 75.4 us  [per_device(): pl.pallas_call(kernel, out_shape=(jax.ShapeDtypeStruct((TR, TC, C), BF16)...]
    dot_general x6 -> x0, matrix products: 68 us -> none  [the longest x1 26.6 us: attend(): jnp.einsum(pattern + 'hd,' + key_pattern + 'hd->' + score_form, query_par...]
    all_to_all x2 -> x0, blocking collectives: 56 us -> none  [the longest x1 34.3 us: per_device(): lax.all_to_all(ordered, ('row', 'col'), split_axis=0, concat_axis=0, tile...]
    ppermute x4 -> x0, waiting for transfers between devices: 14.8 us -> none  [the longest x2 7.76 us: extended(): lax.ppermute(head, axis, [((i + 1) % count, i) for i in range(ends)])]
    convert_element_type x4 -> x1, other arithmetic: 15 us -> 2.43 us  [per_device(): (after_conv.astype(F32) + attended.reshape(after_conv.shape).astype(F32))...]
    ppermute x4 -> x0, starting transfers between devices: 7.38 us -> none  [the longest x2 4.8 us: extended(): lax.ppermute(tail, axis, [(i, (i + 1) % count) for i in range(ends)])]
    another operation x3 -> x0, local copies, waits for them, and re-layouts: 7 us -> none  [the longest x1 2.37 us: per_device(): tile_view.transpose(1, 4, 0, 2, 3, 5, 6)]
    convert_element_type x2 -> x0, local copies, waits for them, and re-layouts: 6.41 us -> none  [the longest x1 3.93 us: attend(): mixed = mixed.astype(jnp.bfloat16)]
  transfers between devices with their start and end apart: 4 -> 0, of which waited for: 3 -> 0; matrix products, arithmetic and copies ran while one was open for 0% -> 0% of each run, Pallas kernels for 0% -> 0%
where the time goes in v1:
time: 87.1 us; the launch traced here: 86.8 us
  Pallas kernels  75.4 us (87%)
  local copies, waits for them, and re-layouts  8.95 us (10%)
  other arithmetic  2.43 us (3%)
    pallas_call x1, Pallas kernels, per_device(): pl.pallas_call(kernel, out_shape=(jax.ShapeDtypeStruct((TR, TC, C), BF16)...  75.4 us
    reshape x7, local copies, waits for them, and re-layouts, per_device(): row = lambda v: v.reshape(1, -1)  8.95 us
    convert_element_type x1, other arithmetic, per_device(): (after_conv.astype(F32) + attended.reshape(after_conv.shape).astype(F32))...  2.43 us

profile of v1, /device:TPU:0, one launch (start us, length us, event | category | flops | bytes accessed | tf_op | source)
XLA Modules:
  0.0 86.8 jit_solution(16480968571432978430)
XLA Ops:
  0.0 1.3 %reshape.30.nsc_h = f32[1,768]{1,0:T(1,128)} reshape(f32[768]{0:T(1024)} %param.16) | data formatting | bytes 6144 | tf_op jit(solution)/shard_map/reshape | solution.py:356
  1.3 1.3 %reshape.31.nsh_h = f32[1,768]{1,0:T(1,128)} reshape(f32[768]{0:T(1024)} %param.17) | data formatting | bytes 6144 | tf_op jit(solution)/shard_map/reshape | solution.py:356
  2.5 1.3 %reshape.34.bp_h = f32[1,768]{1,0:T(1,128)} reshape(f32[768]{0:T(1024)} %param.23) | data formatting | bytes 6144 | tf_op jit(solution)/shard_map/reshape | solution.py:356
  3.8 1.3 %reshape.35.ag_h = f32[1,768]{1,0:T(1,128)} reshape(f32[768]{0:T(1024)} %param.24) | data formatting | bytes 6144 | tf_op jit(solution)/shard_map/reshape | solution.py:356
  5.1 1.3 %reshape.36.as_h = f32[1,768]{1,0:T(1,128)} reshape(f32[768]{0:T(1024)} %param.25) | data formatting | bytes 6144 | tf_op jit(solution)/shard_map/reshape | solution.py:356
  6.4 1.3 %reshape.38.bo_h = f32[1,768]{1,0:T(1,128)} reshape(f32[768]{0:T(1024)} %param.29) | data formatting | bytes 6144 | tf_op jit(solution)/shard_map/reshape | solution.py:356
  7.6 1.3 %reshape.37.bq_h = f32[1,2304]{1,0:T(1,128)} reshape(f32[2304]{0:T(1024)} %param.27) | data formatting | bytes 18432 | tf_op jit(solution)/shard_map/reshape | solution.py:356
  9.0 75.4 %block.1 = (bf16[8,64,768]{2,1,0:T(8,128)(2,1)}, bf16[64,8,768]{2,1,0:T(8,128)(2,1)}) custom-call(bf16[8,64,768]{2,1,0:T(8,128)(2,1)} %f_hbm.1, f32[1,768]{1,0:T(1,128)} %reshape.30.nsc_h, f32[1,768]{1,0:T(1,128)} %reshape.31.nsh_h, bf16[768,3072]{1,0:T(8,128)(2,1)} %we_h.1, f32[1,3072]{1,0:T(1,128)} %bitcast.7, f32[3,3,3072]{2,1,0:T(4,128)} %dk_h.1, ...), custom_call_target="tpu_custom_call" | custom-call | tf_op jit(solution)/shard_map/block/pallas_call | solution.py:389
  84.3 2.4 %fusion = bf16[8,64,768]{2,1,0:T(8,128)(2,1)} fusion(bf16[8,64,768]{2,1,0:T(8,128)(2,1)} %get-tuple-element.7, bf16[8,64,768]{2,1,0:T(8,128)(2,1)} %bitcast.6), kind=kLoop, calls=%fused_computation.1 | loop fusion | flops 1572864 | bytes 2359296 | tf_op jit(solution)/shard_map/convert_element_type | solution.py:403

commit v2 on v1

--- a/solution.py
+++ b/solution.py
@@ -35,7 +35,7 @@
     f_hbm, nsc_h, nsh_h, we_h, be_h, dk_h, db_h, wp_h, bp_h, ag_h, as_h, wq_h, bq_h, wo_h, bo_h,
     ac_out, ret_out,
     feat, nsc, nsh, we, be, dk, db, wp, bp, ag, ash, wq, bq, wo, bo,
-    xn, top, bot, left, right, corner, xblk, xcol, hid, hl, hr, dwb, send, recv, xp, qkv, mixed, retbuf, ones,
+    xn, top, bot, left, right, corner, xblk, hid, hl, hr, dwb, send, recv, xp, qkv, mixed, retbuf, ones,
     small_sem, feat_sem, we_sem, w_sem, halo_ssem, halo_rsem, a_ssem, a_rsem, b_ssem, b_rsem, out_sem, self_sem,
 ):
     r = lax.axis_index("row")
@@ -96,7 +96,7 @@
         s.wait()
 
     def normalise(v):
-        return (v.astype(F32) * nsc[...] + nsh[...]).astype(BF16)
+        return (v.astype(F32) * nsc[...][None, :] + nsh[...][None, :]).astype(BF16)
 
     def norm_row(h, _):
         xn[pl.ds(pl.multiple_of(h * TC, TC), TC), :] = normalise(feat[h])
@@ -169,16 +169,17 @@
     want = jnp.where(t < 16, want_l, want_r)
     want = jnp.where(tr <= 9, want, -1)
     pick = jnp.where(n == want, 1.0, 0.0).astype(BF16)
-    xcol[...] = jnp.dot(pick, xblk[...], preferred_element_type=F32).astype(BF16)
+    xn[2 * TC : 2 * TC + 32, :] = jnp.dot(
+        pick, xblk[...], preferred_element_type=F32
+    ).astype(BF16)
 
     def halo_chunk(ci, _):
         cols = pl.ds(pl.multiple_of(ci * 256, 256), 256)
-        acc = jnp.dot(xn[0 : 2 * TC, :], we[:, cols], preferred_element_type=F32)
+        acc = jnp.dot(xn[0 : 2 * TC + 32, :], we[:, cols], preferred_element_type=F32)
         g = gelu(acc + be[:, cols])
         hid[0, :, cols] = (g[0:TC] * top_ok).astype(BF16)
         hid[TR + 1, :, cols] = (g[TC : 2 * TC] * bot_ok).astype(BF16)
-        side = jnp.dot(xcol[...], we[:, cols], preferred_element_type=F32)
-        gs = gelu(side + be[:, cols]).astype(BF16).astype(F32)
+        gs = g[2 * TC : 2 * TC + 32].astype(BF16).astype(F32)
         ti = lax.broadcasted_iota(jnp.int32, (16, 256), 0)
         edge = jnp.where(ti == 0, top_ok, jnp.where(ti == 9, bot_ok, 1.0))
         gl = gs[0:16] * (edge * left_ok)
@@ -229,7 +230,7 @@
             return 0
 
         lax.fori_loop(0, E // 128, lane, 0)
-        proj = jnp.dot(dwb[...], wp[...], preferred_element_type=F32) + bp[...]
+        proj = jnp.dot(dwb[...], wp[...], preferred_element_type=F32) + bp[...][None, :]
         f0 = feat[2 * b].astype(F32)
         f1 = feat[2 * b + 1].astype(F32)
         for o, f in ((0, f0), (1, f1)):
@@ -238,7 +239,7 @@
             wide_ac = acb.astype(F32)
             center = wide_ac - jnp.mean(wide_ac, axis=-1, keepdims=True)
             spread = jnp.mean(center * center, axis=-1, keepdims=True)
-            y = (center * lax.rsqrt(spread + 1e-06) * ag[...] + ash[...]).astype(BF16)
+            y = (center * lax.rsqrt(spread + 1e-06) * ag[...][None, :] + ash[...][None, :]).astype(BF16)
             send[pl.ds((2 * b + o) * 8, 8)] = y.reshape(8, 8, C)
 
         def go(j, _):
@@ -278,7 +279,7 @@
             acc = jnp.dot(
                 xp[mb * 256 : (mb + 1) * 256, :], wq[:, cols], preferred_element_type=F32
             )
-            qkv[mb * 256 : (mb + 1) * 256, cols] = (acc + bq[:, cols]).astype(BF16)
+            qkv[mb * 256 : (mb + 1) * 256, cols] = (acc + bq[cols][None, :]).astype(BF16)
         return 0
 
     lax.fori_loop(0, 9, qkv_chunk, 0)
@@ -300,20 +301,26 @@
             krows = pl.ds(pl.multiple_of(g * 64, 64), 64)
             qrows = pl.ds(pl.multiple_of(g * 64 + qb * per, per), per)
             orows = pl.ds(pl.multiple_of(g * per, per), per)
+            es = []
             for quad in range(QUADS):
                 lo = quad * 128
                 q = qkv[qrows, lo : lo + 128]
                 kk = qkv[krows, C + lo : C + lo + 128]
-                vv = qkv[krows, 2 * C + lo : 2 * C + lo + 128]
                 kbd = jnp.concatenate([kk * m for m in masks], axis=0)
-                vbd = jnp.concatenate([vv * m for m in masks], axis=0)
                 s = lax.dot_general(
                     q, kbd, (((1,), (1,)), ((), ())), preferred_element_type=F32
                 )
-                e = jnp.exp2(s * EXP_SCALE)
-                tot = jnp.dot(e.astype(BF16), ones[...], preferred_element_type=F32)
-                probs = (e / tot).astype(BF16)
-                o = jnp.dot(probs, vbd, preferred_element_type=F32)
+                es.append(jnp.exp2(s * EXP_SCALE))
+            e = jnp.concatenate(es, axis=0)
+            tot = jnp.dot(e.astype(BF16), ones[...], preferred_element_type=F32)
+            probs = (e / tot).astype(BF16)
+            for quad in range(QUADS):
+                lo = quad * 128
+                vv = qkv[krows, 2 * C + lo : 2 * C + lo + 128]
+                vbd = jnp.concatenate([vv * m for m in masks], axis=0)
+                o = jnp.dot(
+                    probs[quad * per : (quad + 1) * per], vbd, preferred_element_type=F32
+                )
                 mixed[orows, lo : lo + 128] = o.astype(BF16)
             return 0
 
@@ -323,7 +330,7 @@
         nn = lax.broadcasted_iota(jnp.int32, (rows, rows), 1)
         back = jnp.where(nn == lax.rem(m, 8) * per + m // 8, 1.0, 0.0).astype(BF16)
         mm = jnp.dot(back, mixed[...], preferred_element_type=F32).astype(BF16)
-        y = (jnp.dot(mm, wo[...], preferred_element_type=F32) + bo[...]).astype(BF16)
+        y = (jnp.dot(mm, wo[...], preferred_element_type=F32) + bo[...][None, :]).astype(BF16)
         retbuf[pl.ds(qb * per, per)] = y.reshape(per, 8, C)
 
         def go(j, _):
@@ -353,7 +360,7 @@
     features, norm_scale, norm_shift, expand_weight, expand_bias, depth_kernel, depth_bias,
     project_weight, project_bias, attn_gain, attn_shift, qkv_weight, qkv_bias, out_weight, out_bias,
 ):
-    row = lambda v: v.reshape(1, -1)
+    row = lambda v: v if v.shape[0] % 1024 else v.reshape(1, -1)
     args = (
         features, row(norm_scale), row(norm_shift), expand_weight, row(expand_bias), depth_kernel,
         row(depth_bias), project_weight, row(project_bias), row(attn_gain), row(attn_shift),
@@ -370,7 +377,6 @@
         vm((TR, 8, C), BF16),
         vm((4, 8, C), BF16),
         vm((256, C), BF16),
-        vm((32, C), BF16),
         vm((TR + 2, TC, E), BF16),
         vm((TR, 8, E), F32),
         vm((TR, 8, E), F32),

time: 87.1 us -> 66.7 us (0.77)
  Pallas kernels: 75.4 us -> 64.2 us
  local copies, waits for them, and re-layouts: 8.95 us -> 0 us
    pallas_call x1, Pallas kernels: 75.4 us -> 64.2 us  [per_device(): pl.pallas_call(kernel, out_shape=(jax.ShapeDtypeStruct((TR, TC, C), BF16)...]
    reshape x7 -> x0, local copies, waits for them, and re-layouts: 8.95 us -> none  [per_device(): row = lambda v: v.reshape(1, -1)]
where the time goes in v2:
time: 66.7 us; the launch traced here: 66.6 us
  Pallas kernels  64.2 us (96%)
  other arithmetic  2.43 us (4%)
    pallas_call x1, Pallas kernels, per_device(): pl.pallas_call(kernel, out_shape=(jax.ShapeDtypeStruct((TR, TC, C), BF16)...  64.2 us
    convert_element_type x1, other arithmetic, per_device(): (after_conv.astype(F32) + attended.reshape(after_conv.shape).astype(F32))...  2.43 us

profile of v2, /device:TPU:0, one launch (start us, length us, event | category | flops | bytes accessed | tf_op | source)
XLA Modules:
  0.0 66.6 jit_solution(14081295242667705224)
XLA Ops:
  0.0 64.2 %block.1 = (bf16[8,64,768]{2,1,0:T(8,128)(2,1)}, bf16[64,8,768]{2,1,0:T(8,128)(2,1)}) custom-call(bf16[8,64,768]{2,1,0:T(8,128)(2,1)} %f_hbm.1, f32[768]{0:T(1024)} %nsc_h.1, f32[768]{0:T(1024)} %nsh_h.1, bf16[768,3072]{1,0:T(8,128)(2,1)} %we_h.1, f32[1,3072]{1,0:T(1,128)} %bitcast.7, f32[3,3,3072]{2,1,0:T(4,128)} %dk_h.1, f32[1,3072]{1,0:T(1,128)} %bitcast.8, ...), custom_call_target="tpu_custom_call" | custom-call | tf_op jit(solution)/shard_map/block/pallas_call | solution.py:395
  64.2 2.4 %fusion = bf16[8,64,768]{2,1,0:T(8,128)(2,1)} fusion(bf16[8,64,768]{2,1,0:T(8,128)(2,1)} %get-tuple-element.7, bf16[8,64,768]{2,1,0:T(8,128)(2,1)} %bitcast.6), kind=kLoop, calls=%fused_computation.1 | loop fusion | flops 1572864 | bytes 2359296 | tf_op jit(solution)/shard_map/convert_element_type | solution.py:409

commit v3 on v2

--- a/solution.py
+++ b/solution.py
@@ -19,7 +19,9 @@
 E = 3072
 HEAD_DIM = 32
 QUADS = 6
-NQ = 2
+NSUB = 2
+PER = 8 // NSUB
+PER_BITS = PER.bit_length() - 1
 WCHUNKS = 6
 GC1 = math.sqrt(2.0 / math.pi)
 GC2 = GC1 * 0.044715
@@ -35,7 +37,7 @@
     f_hbm, nsc_h, nsh_h, we_h, be_h, dk_h, db_h, wp_h, bp_h, ag_h, as_h, wq_h, bq_h, wo_h, bo_h,
     ac_out, ret_out,
     feat, nsc, nsh, we, be, dk, db, wp, bp, ag, ash, wq, bq, wo, bo,
-    xn, top, bot, left, right, corner, xblk, hid, hl, hr, dwb, send, recv, xp, qkv, mixed, retbuf, ones,
+    xn, top, bot, left, right, corner, xblk, hid, hl, hr, dwb, send, recv, xp, qkv, mixed, retbuf, acc, ones,
     small_sem, feat_sem, we_sem, w_sem, halo_ssem, halo_rsem, a_ssem, a_rsem, b_ssem, b_rsem, out_sem, self_sem,
 ):
     r = lax.axis_index("row")
@@ -207,30 +209,42 @@
     def block(k, _):
         b = lax.rem(k + me, 4)
 
+        def depthwise(ci):
+            for half in range(2):
+                cols = pl.ds(pl.multiple_of(ci * 256 + half * 128, 128), 128)
+                rows = [hid[2 * b + i, :, cols].astype(F32) for i in range(4)]
+                bias = db[:, cols]
+                taps = [[dk[a, q : q + 1, cols] for q in range(3)] for a in range(3)]
+                for o in range(2):
+                    s = [
+                        rows[o] * taps[0][q] + rows[o + 1] * taps[1][q] + rows[o + 2] * taps[2][q]
+                        for q in range(3)
+                    ]
+                    down = pltpu.roll(s[0], 1, 0)
+                    up = pltpu.roll(s[2], TC - 1, 0)
+                    first = jnp.where(sub_id == 0, hl[2 * b + o, :, cols], down[0:8])
+                    last = jnp.where(sub_id == 7, hr[2 * b + o, :, cols], up[TC - 8 : TC])
+                    total = (
+                        s[1] + bias
+                        + jnp.concatenate([first, down[8:TC]], axis=0)
+                        + jnp.concatenate([up[0 : TC - 8], last], axis=0)
+                    )
+                    dwb[o * TC : (o + 1) * TC, cols] = gelu(total).astype(BF16)
+
+        def project(ci):
+            part = pl.ds(pl.multiple_of(ci * 256, 256), 256)
+            acc[...] += jnp.dot(dwb[:, part], wp[part, :], preferred_element_type=F32)
+
         def lane(ci, _):
-            cols = pl.ds(pl.multiple_of(ci * 128, 128), 128)
-            rows = [hid[2 * b + i, :, cols].astype(F32) for i in range(4)]
-            bias = db[:, cols]
-            taps = [[dk[a, q : q + 1, cols] for q in range(3)] for a in range(3)]
-            for o in range(2):
-                s = [
-                    rows[o] * taps[0][q] + rows[o + 1] * taps[1][q] + rows[o + 2] * taps[2][q]
-                    for q in range(3)
-                ]
-                down = pltpu.roll(s[0], 1, 0)
-                up = pltpu.roll(s[2], TC - 1, 0)
-                first = jnp.where(sub_id == 0, hl[2 * b + o, :, cols], down[0:8])
-                last = jnp.where(sub_id == 7, hr[2 * b + o, :, cols], up[TC - 8 : TC])
-                total = (
-                    s[1] + bias
-                    + jnp.concatenate([first, down[8:TC]], axis=0)
-                    + jnp.concatenate([up[0 : TC - 8], last], axis=0)
-                )
-                dwb[o * TC : (o + 1) * TC, cols] = gelu(total).astype(BF16)
+            project(ci - 1)
+            depthwise(ci)
             return 0
 
-        lax.fori_loop(0, E // 128, lane, 0)
-        proj = jnp.dot(dwb[...], wp[...], preferred_element_type=F32) + bp[...][None, :]
+        acc[...] = jnp.broadcast_to(bp[...][None, :], (2 * TC, C))
+        depthwise(0)
+        lax.fori_loop(1, E // 256, lane, 0)
+        project(E // 256 - 1)
+        proj = acc[...]
         f0 = feat[2 * b].astype(F32)
         f1 = feat[2 * b + 1].astype(F32)
         for o, f in ((0, f0), (1, f1)):
@@ -258,54 +272,48 @@
     accopy = pltpu.make_async_copy(feat, ac_out, out_sem)
     accopy.start()
     recv[pl.ds(me, 1)] = send[pl.ds(me, 1)]
-    ri = lax.broadcasted_iota(jnp.int32, (256, 256), 0) // 64
-    rj = lax.broadcasted_iota(jnp.int32, (256, 256), 1) // 64
+    ri = lax.broadcasted_iota(jnp.int32, (256, 256), 0) >> 6
+    rj = lax.broadcasted_iota(jnp.int32, (256, 256), 1) >> 6
     ones[...] = jnp.where(ri == rj, 1.0, 0.0).astype(BF16)
     bigs[1].wait()
     bigs[2].wait()
     pltpu.make_async_copy(send.at[pl.ds(0, PEERS - 1)], send.at[pl.ds(0, PEERS - 1)], a_ssem).wait()
     pltpu.make_async_copy(recv.at[pl.ds(0, PEERS - 1)], recv.at[pl.ds(0, PEERS - 1)], a_rsem).wait()
 
-    x = recv[...].reshape(TOKENS, C)
-    for mb in range(2):
-        m = lax.broadcasted_iota(jnp.int32, (256, TOKENS), 0) + mb * 256
-        nn = lax.broadcasted_iota(jnp.int32, (256, TOKENS), 1)
-        perm = jnp.where(nn == lax.rem(m, 64) * 8 + m // 64, 1.0, 0.0).astype(BF16)
-        xp[mb * 256 : (mb + 1) * 256, :] = jnp.dot(perm, x, preferred_element_type=F32).astype(BF16)
-
-    def qkv_chunk(ci, _):
-        cols = pl.ds(pl.multiple_of(ci * 256, 256), 256)
-        for mb in range(2):
-            acc = jnp.dot(
-                xp[mb * 256 : (mb + 1) * 256, :], wq[:, cols], preferred_element_type=F32
-            )
-            qkv[mb * 256 : (mb + 1) * 256, cols] = (acc + bq[cols][None, :]).astype(BF16)
-        return 0
-
-    lax.fori_loop(0, 9, qkv_chunk, 0)
-
-    per = PEERS // NQ
-    lane_head = lax.broadcasted_iota(jnp.int32, (64, 128), 1) // HEAD_DIM
+    lane_head = lax.broadcasted_iota(jnp.int32, (64, 128), 1) >> 5
     masks = [jnp.where(lane_head == i, 1.0, 0.0).astype(BF16) for i in range(4)]
 
-    def return_chunk(p):
+    def return_chunk(p, sub):
         return pltpu.make_async_remote_copy(
-            src_ref=retbuf.at[p], dst_ref=ret_out.at[me], send_sem=b_ssem, recv_sem=b_rsem,
-            device_id=place(p), device_id_type=MESH,
-        )
-
-    def query_block(qq, _):
-        qb = lax.rem(qq + me, NQ)
+            src_ref=retbuf.at[sub, p], dst_ref=ret_out.at[me, pl.ds(PER * sub, PER)],
+            send_sem=b_ssem, recv_sem=b_rsem, device_id=place(p), device_id_type=MESH,
+        )
+
+    subrows = PER * PEERS
+
+    for sub in range(NSUB):
+        m = lax.broadcasted_iota(jnp.int32, (subrows, TOKENS), 0)
+        nn = lax.broadcasted_iota(jnp.int32, (subrows, TOKENS), 1)
+        perm = jnp.where(nn == (m & 63) * 8 + (m >> 6) + PER * sub, 1.0, 0.0).astype(BF16)
+        xp[...] = jnp.dot(
+            perm, recv[...].reshape(TOKENS, C), preferred_element_type=F32
+        ).astype(BF16)
+
+        def qkv_chunk(ci, _):
+            cols = pl.ds(pl.multiple_of(ci * 256, 256), 256)
+            part = jnp.dot(xp[...], wq[:, cols], preferred_element_type=F32)
+            qkv[:, cols] = (part + bq[cols][None, :]).astype(BF16)
+            return 0
+
+        lax.fori_loop(0, 9, qkv_chunk, 0)
 
         def group(g, _):
-            krows = pl.ds(pl.multiple_of(g * 64, 64), 64)
-            qrows = pl.ds(pl.multiple_of(g * 64 + qb * per, per), per)
-            orows = pl.ds(pl.multiple_of(g * per, per), per)
+            rows = pl.ds(pl.multiple_of(g * 64, 64), 64)
             es = []
             for quad in range(QUADS):
                 lo = quad * 128
-                q = qkv[qrows, lo : lo + 128]
-                kk = qkv[krows, C + lo : C + lo + 128]
+                q = qkv[rows, lo : lo + 128]
+                kk = qkv[rows, C + lo : C + lo + 128]
                 kbd = jnp.concatenate([kk * m for m in masks], axis=0)
                 s = lax.dot_general(
                     q, kbd, (((1,), (1,)), ((), ())), preferred_element_type=F32
@@ -316,44 +324,40 @@
             probs = (e / tot).astype(BF16)
             for quad in range(QUADS):
                 lo = quad * 128
-                vv = qkv[krows, 2 * C + lo : 2 * C + lo + 128]
+                vv = qkv[rows, 2 * C + lo : 2 * C + lo + 128]
                 vbd = jnp.concatenate([vv * m for m in masks], axis=0)
                 o = jnp.dot(
-                    probs[quad * per : (quad + 1) * per], vbd, preferred_element_type=F32
+                    probs[quad * 64 : (quad + 1) * 64], vbd, preferred_element_type=F32
                 )
-                mixed[orows, lo : lo + 128] = o.astype(BF16)
+                mixed[rows, lo : lo + 128] = o.astype(BF16)
             return 0
 
-        lax.fori_loop(0, 8, group, 0)
-        rows = per * 8
-        m = lax.broadcasted_iota(jnp.int32, (rows, rows), 0)
-        nn = lax.broadcasted_iota(jnp.int32, (rows, rows), 1)
-        back = jnp.where(nn == lax.rem(m, 8) * per + m // 8, 1.0, 0.0).astype(BF16)
+        lax.fori_loop(0, PER, group, 0)
+        m = lax.broadcasted_iota(jnp.int32, (subrows, subrows), 0)
+        nn = lax.broadcasted_iota(jnp.int32, (subrows, subrows), 1)
+        back = jnp.where(
+            nn == (m & (PER - 1)) * 64 + (m >> PER_BITS), 1.0, 0.0
+        ).astype(BF16)
         mm = jnp.dot(back, mixed[...], preferred_element_type=F32).astype(BF16)
         y = (jnp.dot(mm, wo[...], preferred_element_type=F32) + bo[...][None, :]).astype(BF16)
-        retbuf[pl.ds(qb * per, per)] = y.reshape(per, 8, C)
+        retbuf[sub] = y.reshape(PEERS, PER, C)
+        pltpu.make_async_copy(
+            retbuf.at[sub, me], ret_out.at[me, pl.ds(PER * sub, PER)], self_sem.at[sub]
+        ).start()
 
         def go(j, _):
-            p = per * qb + lax.rem(j + me, per)
-
-            @pl.when(p != me)
-            def _():
-                return_chunk(p).start()
-
+            return_chunk(lax.rem(j + me, PEERS), sub).start()
             return 0
 
-        lax.fori_loop(0, per, go, 0)
-        return 0
-
-    lax.fori_loop(0, NQ, query_block, 0)
-    own = pltpu.make_async_copy(retbuf.at[me], ret_out.at[me], self_sem)
-    own.start()
-    own.wait()
+        lax.fori_loop(1, PEERS, go, 0)
+
+    for sub in range(NSUB):
+        pltpu.make_async_copy(
+            retbuf.at[sub, me], ret_out.at[me, pl.ds(PER * sub, PER)], self_sem.at[sub]
+        ).wait()
     accopy.wait()
-    pltpu.make_async_copy(retbuf.at[pl.ds(0, PEERS - 1)], retbuf.at[pl.ds(0, PEERS - 1)], b_ssem).wait()
-    pltpu.make_async_copy(
-        ret_out.at[pl.ds(0, PEERS - 1)], ret_out.at[pl.ds(0, PEERS - 1)], b_rsem
-    ).wait()
+    pltpu.make_async_copy(ret_out.at[pl.ds(0, PEERS - 1)], ret_out.at[pl.ds(0, PEERS - 1)], b_ssem).wait()
+    pltpu.make_async_copy(ret_out.at[pl.ds(0, PEERS - 1)], ret_out.at[pl.ds(0, PEERS - 1)], b_rsem).wait()
 
 
 def per_device(
@@ -383,13 +387,14 @@
         vm((2 * TC, E), BF16),
         vm((PEERS, 8, C), BF16),
         vm((PEERS, 8, C), BF16),
-        vm((TOKENS, C), BF16),
-        vm((TOKENS, 3 * C), BF16),
-        vm((TOKENS // NQ, C), BF16),
-        vm((PEERS, 8, C), BF16),
+        vm((TOKENS // NSUB, C), BF16),
+        vm((TOKENS // NSUB, 3 * C), BF16),
+        vm((TOKENS // NSUB, C), BF16),
+        vm((NSUB, PEERS, PER, C), BF16),
+        vm((2 * TC, C), F32),
         vm((256, 256), BF16),
         dma((10,)), dma, dma((WCHUNKS,)), dma((3,)), dma((8,)), dma((8,)),
-        dma, dma, dma, dma, dma, dma,
+        dma, dma, dma, dma, dma, dma((NSUB,)),
     ]
     hbm = pl.BlockSpec(memory_space=pl.ANY)
     after_conv, attended = pl.pallas_call(

time: 66.7 us -> 66.6 us (level)
  no operation moved by 1% of the time
where the time goes in v3:
time: 66.6 us; the launch traced here: 66.4 us
  Pallas kernels  64 us (96%)
  other arithmetic  2.43 us (4%)
    pallas_call x1, Pallas kernels, per_device(): pl.pallas_call(kernel, out_shape=(jax.ShapeDtypeStruct((TR, TC, C), BF16)...  64 us
    convert_element_type x1, other arithmetic, per_device(): (after_conv.astype(F32) + attended.reshape(after_conv.shape).astype(F32))...  2.43 us

profile of v3, /device:TPU:0, one launch (start us, length us, event | category | flops | bytes accessed | tf_op | source)
XLA Modules:
  0.0 66.4 jit_solution(14841677721495894672)
XLA Ops:
  0.0 64.0 %block.1 = (bf16[8,64,768]{2,1,0:T(8,128)(2,1)}, bf16[64,8,768]{2,1,0:T(8,128)(2,1)}) custom-call(bf16[8,64,768]{2,1,0:T(8,128)(2,1)} %f_hbm.1, f32[768]{0:T(1024)} %nsc_h.1, f32[768]{0:T(1024)} %nsh_h.1, bf16[768,3072]{1,0:T(8,128)(2,1)} %we_h.1, f32[1,3072]{1,0:T(1,128)} %bitcast.7, f32[3,3,3072]{2,1,0:T(4,128)} %dk_h.1, f32[1,3072]{1,0:T(1,128)} %bitcast.8, ...), custom_call_target="tpu_custom_call" | custom-call | tf_op jit(solution)/shard_map/block/pallas_call | solution.py:400
  64.0 2.4 %fusion = bf16[8,64,768]{2,1,0:T(8,128)(2,1)} fusion(bf16[8,64,768]{2,1,0:T(8,128)(2,1)} %get-tuple-element.7, bf16[8,64,768]{2,1,0:T(8,128)(2,1)} %bitcast.6), kind=kLoop, calls=%fused_computation.1 | loop fusion | flops 1572864 | bytes 2359296 | tf_op jit(solution)/shard_map/convert_element_type | solution.py:414

commit v4 on v3

--- a/solution.py
+++ b/solution.py
@@ -42,11 +42,14 @@
 ):
     r = lax.axis_index("row")
     c = lax.axis_index("col")
-    core = lax.rem(c, 2)
-    me = r * 8 + c // 2
-
-    def place(p):
-        return (p // 8, 2 * lax.rem(p, 8) + core)
+    core = c & 1
+    x, y, z = r & 3, ((r >> 2) << 1) + ((c >> 1) & 1), c >> 2
+    me = (((x + y + z) & 3) << 4) + (y << 2) + z
+
+    def place(k):
+        y, z = (k >> 2) & 3, k & 3
+        x = ((k >> 4) - y - z) & 3
+        return (((y >> 1) << 2) + x, (z << 2) + ((y & 1) << 1) + core)
 
     bar = pltpu.get_barrier_semaphore()
 
@@ -119,7 +122,7 @@
     early = 4
     for i in range(early):
         wcopies[i].wait()
-        lax.fori_loop(2 * i, 2 * i + 2, expand_chunk, 0)
+        lax.fori_loop(2 * i, 2 * i + 2, expand_chunk, 0, unroll=2)
 
     pl.semaphore_wait(bar, PEERS - 1 + 6)
 
@@ -145,7 +148,7 @@
 
     for i in range(early, WCHUNKS):
         wcopies[i].wait()
-        lax.fori_loop(2 * i, 2 * i + 2, expand_chunk, 0)
+        lax.fori_loop(2 * i, 2 * i + 2, expand_chunk, 0, unroll=2)
 
     for h in halos:
         h.wait()
@@ -195,7 +198,7 @@
             hr[i, :, cols] = jnp.broadcast_to(redge[i : i + 1], (8, 256))
         return 0
 
-    lax.fori_loop(0, E // 256, halo_chunk, 0)
+    lax.fori_loop(0, E // 256, halo_chunk, 0, unroll=3)
 
     bigs[0].wait()
     sub_id = lax.broadcasted_iota(jnp.int32, (8, 128), 0)
@@ -207,7 +210,7 @@
         )
 
     def block(k, _):
-        b = lax.rem(k + me, 4)
+        b = (k + (me >> 4)) & 3
 
         def depthwise(ci):
             for half in range(2):
@@ -265,7 +268,7 @@
 
             return 0
 
-        lax.fori_loop(0, 16, go, 0)
+        lax.fori_loop(0, 16, go, 0, unroll=8)
         return 0
 
     lax.fori_loop(0, 4, block, 0)
@@ -303,9 +306,12 @@
             cols = pl.ds(pl.multiple_of(ci * 256, 256), 256)
             part = jnp.dot(xp[...], wq[:, cols], preferred_element_type=F32)
             qkv[:, cols] = (part + bq[cols][None, :]).astype(BF16)
+            if sub > 0:
+                for j in range(7):
+                    return_chunk((ci * 7 + j + 1 + me) & (PEERS - 1), sub - 1).start()
             return 0
 
-        lax.fori_loop(0, 9, qkv_chunk, 0)
+        lax.fori_loop(0, 9, qkv_chunk, 0, unroll=9)
 
         def group(g, _):
             rows = pl.ds(pl.multiple_of(g * 64, 64), 64)
@@ -332,7 +338,7 @@
                 mixed[rows, lo : lo + 128] = o.astype(BF16)
             return 0
 
-        lax.fori_loop(0, PER, group, 0)
+        lax.fori_loop(0, PER, group, 0, unroll=4)
         m = lax.broadcasted_iota(jnp.int32, (subrows, subrows), 0)
         nn = lax.broadcasted_iota(jnp.int32, (subrows, subrows), 1)
         back = jnp.where(
@@ -349,7 +355,8 @@
             return_chunk(lax.rem(j + me, PEERS), sub).start()
             return 0
 
-        lax.fori_loop(1, PEERS, go, 0)
+        if sub == NSUB - 1:
+            lax.fori_loop(1, PEERS, go, 0, unroll=21)
 
     for sub in range(NSUB):
         pltpu.make_async_copy(

time: 66.6 us -> 59.6 us (0.89)
  Pallas kernels: 64 us -> 57.1 us
    pallas_call x1, Pallas kernels: 64 us -> 57.1 us  [per_device(): pl.pallas_call(kernel, out_shape=(jax.ShapeDtypeStruct((TR, TC, C), BF16)...]
where the time goes in v4:
time: 59.6 us; the launch traced here: 59.5 us
  Pallas kernels  57.1 us (96%)
  other arithmetic  2.43 us (4%)
    pallas_call x1, Pallas kernels, per_device(): pl.pallas_call(kernel, out_shape=(jax.ShapeDtypeStruct((TR, TC, C), BF16)...  57.1 us
    convert_element_type x1, other arithmetic, per_device(): (after_conv.astype(F32) + attended.reshape(after_conv.shape).astype(F32))...  2.43 us

profile of v4, /device:TPU:0, one launch (start us, length us, event | category | flops | bytes accessed | tf_op | source)
XLA Modules:
  0.0 59.5 jit_solution(9895848635841951932)
XLA Ops:
  0.0 57.1 %block.1 = (bf16[8,64,768]{2,1,0:T(8,128)(2,1)}, bf16[64,8,768]{2,1,0:T(8,128)(2,1)}) custom-call(bf16[8,64,768]{2,1,0:T(8,128)(2,1)} %f_hbm.1, f32[768]{0:T(1024)} %nsc_h.1, f32[768]{0:T(1024)} %nsh_h.1, bf16[768,3072]{1,0:T(8,128)(2,1)} %we_h.1, f32[1,3072]{1,0:T(1,128)} %bitcast.7, f32[3,3,3072]{2,1,0:T(4,128)} %dk_h.1, f32[1,3072]{1,0:T(1,128)} %bitcast.8, ...), custom_call_target="tpu_custom_call" | custom-call | tf_op jit(solution)/shard_map/block/pallas_call | solution.py:407
  57.1 2.4 %fusion = bf16[8,64,768]{2,1,0:T(8,128)(2,1)} fusion(bf16[8,64,768]{2,1,0:T(8,128)(2,1)} %get-tuple-element.7, bf16[8,64,768]{2,1,0:T(8,128)(2,1)} %bitcast.6), kind=kLoop, calls=%fused_computation.1 | loop fusion | flops 1572864 | bytes 2359296 | tf_op jit(solution)/shard_map/convert_element_type | solution.py:421

commit v5 on v4

--- a/solution.py
+++ b/solution.py
@@ -115,11 +115,11 @@
             acc = jnp.dot(
                 xn[mb * 256 : (mb + 1) * 256, :], we[:, cols], preferred_element_type=F32
             )
-            g = gelu(acc + be[:, cols]).astype(BF16)
+            g = gelu((acc + be[:, cols]).astype(BF16))
             hid[1 + 4 * mb : 5 + 4 * mb, :, cols] = g.reshape(4, TC, 256)
         return 0
 
-    early = 4
+    early = 1
     for i in range(early):
         wcopies[i].wait()
         lax.fori_loop(2 * i, 2 * i + 2, expand_chunk, 0, unroll=2)
@@ -136,12 +136,12 @@
     halos = [
         halo(feat.at[TR - 1], top, 0, 1, 0),
         halo(feat.at[0], bot, 1, -1, 0),
-        halo(feat.at[:, pl.ds(TC - 8, 8)], left, 2, 0, 1),
-        halo(feat.at[:, pl.ds(0, 8)], right, 3, 0, -1),
-        halo(feat.at[TR - 1, pl.ds(TC - 8, 8)], corner.at[0], 4, 1, 1),
-        halo(feat.at[0, pl.ds(TC - 8, 8)], corner.at[1], 5, -1, 1),
-        halo(feat.at[TR - 1, pl.ds(0, 8)], corner.at[2], 6, 1, -1),
-        halo(feat.at[0, pl.ds(0, 8)], corner.at[3], 7, -1, -1),
+        halo(feat.at[:, pl.ds(TC - 4, 4)], left.at[:, pl.ds(4, 4)], 2, 0, 1),
+        halo(feat.at[:, pl.ds(0, 4)], right.at[:, pl.ds(0, 4)], 3, 0, -1),
+        halo(feat.at[TR - 1, pl.ds(TC - 4, 4)], corner.at[0, pl.ds(4, 4)], 4, 1, 1),
+        halo(feat.at[0, pl.ds(TC - 4, 4)], corner.at[1, pl.ds(4, 4)], 5, -1, 1),
+        halo(feat.at[TR - 1, pl.ds(0, 4)], corner.at[2, pl.ds(0, 4)], 6, 1, -1),
+        halo(feat.at[0, pl.ds(0, 4)], corner.at[3, pl.ds(0, 4)], 7, -1, -1),
     ]
     for h in halos:
         h.start()
@@ -232,7 +232,7 @@
                         + jnp.concatenate([first, down[8:TC]], axis=0)
                         + jnp.concatenate([up[0 : TC - 8], last], axis=0)
                     )
-                    dwb[o * TC : (o + 1) * TC, cols] = gelu(total).astype(BF16)
+                    dwb[o * TC : (o + 1) * TC, cols] = gelu(total.astype(BF16))
 
         def project(ci):
             part = pl.ds(pl.multiple_of(ci * 256, 256), 256)

time: 59.6 us -> 58.1 us (0.975)
  Pallas kernels: 57.1 us -> 55.6 us
    pallas_call x1, Pallas kernels: 57.1 us -> 55.6 us  [per_device(): pl.pallas_call(kernel, out_shape=(jax.ShapeDtypeStruct((TR, TC, C), BF16)...]
where the time goes in v5:
time: 58.1 us; the launch traced here: 58 us
  Pallas kernels  55.6 us (96%)
  other arithmetic  2.43 us (4%)
    pallas_call x1, Pallas kernels, per_device(): pl.pallas_call(kernel, out_shape=(jax.ShapeDtypeStruct((TR, TC, C), BF16)...  55.6 us
    convert_element_type x1, other arithmetic, per_device(): (after_conv.astype(F32) + attended.reshape(after_conv.shape).astype(F32))...  2.43 us

profile of v5, /device:TPU:0, one launch (start us, length us, event | category | flops | bytes accessed | tf_op | source)
XLA Modules:
  0.0 58.0 jit_solution(8889566202830677089)
XLA Ops:
  0.0 55.6 %block.1 = (bf16[8,64,768]{2,1,0:T(8,128)(2,1)}, bf16[64,8,768]{2,1,0:T(8,128)(2,1)}) custom-call(bf16[8,64,768]{2,1,0:T(8,128)(2,1)} %f_hbm.1, f32[768]{0:T(1024)} %nsc_h.1, f32[768]{0:T(1024)} %nsh_h.1, bf16[768,3072]{1,0:T(8,128)(2,1)} %we_h.1, f32[1,3072]{1,0:T(1,128)} %bitcast.7, f32[3,3,3072]{2,1,0:T(4,128)} %dk_h.1, f32[1,3072]{1,0:T(1,128)} %bitcast.8, ...), custom_call_target="tpu_custom_call" | custom-call | tf_op jit(solution)/shard_map/block/pallas_call | solution.py:407
  55.6 2.4 %fusion = bf16[8,64,768]{2,1,0:T(8,128)(2,1)} fusion(bf16[8,64,768]{2,1,0:T(8,128)(2,1)} %get-tuple-element.7, bf16[8,64,768]{2,1,0:T(8,128)(2,1)} %bitcast.6), kind=kLoop, calls=%fused_computation.1 | loop fusion | flops 1572864 | bytes 2359296 | tf_op jit(solution)/shard_map/convert_element_type | solution.py:421

commit v6 on v5

--- a/solution.py
+++ b/solution.py
@@ -80,7 +80,7 @@
         )
         return 0
 
-    lax.fori_loop(1, PEERS, signal, 0)
+    lax.fori_loop(1, PEERS, signal, 0, unroll=9)
     for dr in (-1, 0, 1):
         for dc in (-1, 1):
             pl.semaphore_signal(
@@ -89,40 +89,40 @@
                 device_id_type=MESH,
             )
 
+    fcopy.wait()
+    for s in smalls:
+        s.wait()
+
+    def normalise(v):
+        return (v.astype(F32) * nsc[...][None, :] + nsh[...][None, :]).astype(BF16)
+
+    def norm_row(h, _):
+        xn[pl.ds(pl.multiple_of(h * TC, TC), TC), :] = normalise(feat[h])
+        return 0
+
+    lax.fori_loop(0, TR, norm_row, 0)
+
+    def expand_chunk(ci, _):
+        cols = pl.ds(pl.multiple_of(ci * 256, 256), 256)
+        for mb in range(2):
+            acc = jnp.dot(
+                xn[mb * 256 : (mb + 1) * 256, :], we[:, cols], preferred_element_type=F32
+            )
+            g = gelu(acc + be[:, cols]).astype(BF16)
+            hid[1 + 4 * mb : 5 + 4 * mb, :, cols] = g.reshape(4, TC, 256)
+        return 0
+
+    early = 1
+    for i in range(early):
+        wcopies[i].wait()
+        lax.fori_loop(2 * i, 2 * i + 2, expand_chunk, 0, unroll=2)
+
     bigs = [
         pltpu.make_async_copy(s, d, w_sem.at[i])
         for i, (s, d) in enumerate(((wp_h, wp), (wq_h, wq), (wo_h, wo)))
     ]
     for w in bigs:
         w.start()
-
-    fcopy.wait()
-    for s in smalls:
-        s.wait()
-
-    def normalise(v):
-        return (v.astype(F32) * nsc[...][None, :] + nsh[...][None, :]).astype(BF16)
-
-    def norm_row(h, _):
-        xn[pl.ds(pl.multiple_of(h * TC, TC), TC), :] = normalise(feat[h])
-        return 0
-
-    lax.fori_loop(0, TR, norm_row, 0)
-
-    def expand_chunk(ci, _):
-        cols = pl.ds(pl.multiple_of(ci * 256, 256), 256)
-        for mb in range(2):
-            acc = jnp.dot(
-                xn[mb * 256 : (mb + 1) * 256, :], we[:, cols], preferred_element_type=F32
-            )
-            g = gelu((acc + be[:, cols]).astype(BF16))
-            hid[1 + 4 * mb : 5 + 4 * mb, :, cols] = g.reshape(4, TC, 256)
-        return 0
-
-    early = 1
-    for i in range(early):
-        wcopies[i].wait()
-        lax.fori_loop(2 * i, 2 * i + 2, expand_chunk, 0, unroll=2)
 
     pl.semaphore_wait(bar, PEERS - 1 + 6)
 
@@ -339,24 +339,34 @@
             return 0
 
         lax.fori_loop(0, PER, group, 0, unroll=4)
-        m = lax.broadcasted_iota(jnp.int32, (subrows, subrows), 0)
-        nn = lax.broadcasted_iota(jnp.int32, (subrows, subrows), 1)
-        back = jnp.where(
-            nn == (m & (PER - 1)) * 64 + (m >> PER_BITS), 1.0, 0.0
-        ).astype(BF16)
-        mm = jnp.dot(back, mixed[...], preferred_element_type=F32).astype(BF16)
-        y = (jnp.dot(mm, wo[...], preferred_element_type=F32) + bo[...][None, :]).astype(BF16)
-        retbuf[sub] = y.reshape(PEERS, PER, C)
+        parts = 2 if sub == NSUB - 1 else 1
+        span, peers = subrows // parts, PEERS // parts
+        m = lax.broadcasted_iota(jnp.int32, (span, subrows), 0)
+        nn = lax.broadcasted_iota(jnp.int32, (span, subrows), 1)
+        for part in range(parts):
+            which = (part + me) & (parts - 1)
+            token = m + which * span
+            back = jnp.where(
+                nn == (token & (PER - 1)) * 64 + (token >> PER_BITS), 1.0, 0.0
+            ).astype(BF16)
+            mm = jnp.dot(back, mixed[...], preferred_element_type=F32).astype(BF16)
+            y = (jnp.dot(mm, wo[...], preferred_element_type=F32) + bo[...][None, :]).astype(BF16)
+            retbuf[sub, pl.ds(which * peers, peers)] = y.reshape(peers, PER, C)
+
+            def go(j, _):
+                p = which * peers + ((j + me) & (peers - 1))
+
+                @pl.when(p != me)
+                def _():
+                    return_chunk(p, sub).start()
+
+                return 0
+
+            if sub == NSUB - 1:
+                lax.fori_loop(0, peers, go, 0, unroll=8)
         pltpu.make_async_copy(
             retbuf.at[sub, me], ret_out.at[me, pl.ds(PER * sub, PER)], self_sem.at[sub]
         ).start()
-
-        def go(j, _):
-            return_chunk(lax.rem(j + me, PEERS), sub).start()
-            return 0
-
-        if sub == NSUB - 1:
-            lax.fori_loop(1, PEERS, go, 0, unroll=21)
 
     for sub in range(NSUB):
         pltpu.make_async_copy(

time: 58.1 us -> 57.4 us (0.988)
  Pallas kernels: 55.6 us -> 54.9 us
    pallas_call x1, Pallas kernels: 55.6 us -> 54.9 us  [per_device(): pl.pallas_call(kernel, out_shape=(jax.ShapeDtypeStruct((TR, TC, C), BF16)...]
where the time goes in v6:
time: 57.4 us; the launch traced here: 57.3 us
  Pallas kernels  54.9 us (96%)
  other arithmetic  2.43 us (4%)
    pallas_call x1, Pallas kernels, per_device(): pl.pallas_call(kernel, out_shape=(jax.ShapeDtypeStruct((TR, TC, C), BF16)...  54.9 us
    convert_element_type x1, other arithmetic, per_device(): (after_conv.astype(F32) + attended.reshape(after_conv.shape).astype(F32))...  2.43 us

profile of v6, /device:TPU:0, one launch (start us, length us, event | category | flops | bytes accessed | tf_op | source)
XLA Modules:
  0.0 57.3 jit_solution(15322012902165567785)
XLA Ops:
  0.0 54.9 %block.1 = (bf16[8,64,768]{2,1,0:T(8,128)(2,1)}, bf16[64,8,768]{2,1,0:T(8,128)(2,1)}) custom-call(bf16[8,64,768]{2,1,0:T(8,128)(2,1)} %f_hbm.1, f32[768]{0:T(1024)} %nsc_h.1, f32[768]{0:T(1024)} %nsh_h.1, bf16[768,3072]{1,0:T(8,128)(2,1)} %we_h.1, f32[1,3072]{1,0:T(1,128)} %bitcast.7, f32[3,3,3072]{2,1,0:T(4,128)} %dk_h.1, f32[1,3072]{1,0:T(1,128)} %bitcast.8, ...), custom_call_target="tpu_custom_call" | custom-call | tf_op jit(solution)/shard_map/block/pallas_call | solution.py:417
  54.9 2.4 %fusion = bf16[8,64,768]{2,1,0:T(8,128)(2,1)} fusion(bf16[8,64,768]{2,1,0:T(8,128)(2,1)} %get-tuple-element.7, bf16[8,64,768]{2,1,0:T(8,128)(2,1)} %bitcast.6), kind=kLoop, calls=%fused_computation.1 | loop fusion | flops 1572864 | bytes 2359296 | tf_op jit(solution)/shard_map/convert_element_type | solution.py:431

commit v7 on v6

--- a/solution.py
+++ b/solution.py
@@ -198,7 +198,7 @@
             hr[i, :, cols] = jnp.broadcast_to(redge[i : i + 1], (8, 256))
         return 0
 
-    lax.fori_loop(0, E // 256, halo_chunk, 0, unroll=3)
+    lax.fori_loop(0, E // 256, halo_chunk, 0, unroll=6)
 
     bigs[0].wait()
     sub_id = lax.broadcasted_iota(jnp.int32, (8, 128), 0)
@@ -268,7 +268,7 @@
 
             return 0
 
-        lax.fori_loop(0, 16, go, 0, unroll=8)
+        lax.fori_loop(0, 16, go, 0, unroll=16)
         return 0
 
     lax.fori_loop(0, 4, block, 0)
@@ -363,7 +363,7 @@
                 return 0
 
             if sub == NSUB - 1:
-                lax.fori_loop(0, peers, go, 0, unroll=8)
+                lax.fori_loop(0, peers, go, 0, unroll=32)
         pltpu.make_async_copy(
             retbuf.at[sub, me], ret_out.at[me, pl.ds(PER * sub, PER)], self_sem.at[sub]
         ).start()

time: 57.4 us -> 57.1 us (level)
  no operation moved by 1% of the time
where the time goes in v7:
time: 57.1 us; the launch traced here: 57 us
  Pallas kernels  54.5 us (95%)
  other arithmetic  2.43 us (4%)
    pallas_call x1, Pallas kernels, per_device(): pl.pallas_call(kernel, out_shape=(jax.ShapeDtypeStruct((TR, TC, C), BF16)...  54.5 us
    convert_element_type x1, other arithmetic, per_device(): (after_conv.astype(F32) + attended.reshape(after_conv.shape).astype(F32))...  2.43 us

profile of v7, /device:TPU:0, one launch (start us, length us, event | category | flops | bytes accessed | tf_op | source)
XLA Modules:
  0.0 57.0 jit_solution(90036810844728973)
XLA Ops:
  0.0 54.5 %block.1 = (bf16[8,64,768]{2,1,0:T(8,128)(2,1)}, bf16[64,8,768]{2,1,0:T(8,128)(2,1)}) custom-call(bf16[8,64,768]{2,1,0:T(8,128)(2,1)} %f_hbm.1, f32[768]{0:T(1024)} %nsc_h.1, f32[768]{0:T(1024)} %nsh_h.1, bf16[768,3072]{1,0:T(8,128)(2,1)} %we_h.1, f32[1,3072]{1,0:T(1,128)} %bitcast.7, f32[3,3,3072]{2,1,0:T(4,128)} %dk_h.1, f32[1,3072]{1,0:T(1,128)} %bitcast.8, ...), custom_call_target="tpu_custom_call" | custom-call | tf_op jit(solution)/shard_map/block/pallas_call | solution.py:417
  54.5 2.4 %fusion = bf16[8,64,768]{2,1,0:T(8,128)(2,1)} fusion(bf16[8,64,768]{2,1,0:T(8,128)(2,1)} %get-tuple-element.7, bf16[8,64,768]{2,1,0:T(8,128)(2,1)} %bitcast.6), kind=kLoop, calls=%fused_computation.1 | loop fusion | flops 1572864 | bytes 2359296 | tf_op jit(solution)/shard_map/convert_element_type | solution.py:431
